TPU v7x, 32 devices: a whole 2x2x4 slice. The times are simulated.
32 devices in a mesh: leaf: 32 (over z, y, x, core).
Axes of the slice: x: 2, y: 2, z: 4, core: 2. Of those that a mesh axis runs over, the one named last changes fastest.
Arguments:
- points: float32 [3, 131072], P(None, 'leaf'), may hold values from 0 to 1
- rhs: float32 [16, 131072], P(None, 'leaf'), may hold values from -6 to 6
- leaf_basis: float32 [32, 131072], P(None, 'leaf'), may hold values from -0.75 to 0.75
- transfer: float32 [32, 32, 2688], P(None, None, 'leaf'), may hold values from -0.5 to 0.5
- proxies: float32 [3, 32, 2720], P(None, None, 'leaf'), may hold values from 0 to 1
- near_list: int32 [2048, 5], P('leaf'), may hold values from -1 to 2047, as said below
- couple_list: int32 [2688, 20], P('leaf'), may hold values from -1 to 2047, as said below
- root_list: int32 [32, 32], P('leaf'), may hold values from -1 to 31, as said below
Outputs:
- product: float32 [16, 131072], P(None, 'leaf')
Inputs may be any that keep to these rules, and one draw needn't show every extreme that they name: `near_list`: entry [t, j] is the leaf t + j - 2 if the block of leaves t and t + j - 2 is near, else -1; every leaf is near itself. Nearness is defined level by level: at level 0 roots t and s are near when they differ by at most a per-root reach of 1 to 2 (the larger of the two); below, two clusters are near when their parents are near and they differ by at most the larger of their reaches. Near leaf blocks, with the coupled pairs of the other two lists, cover every pair of points exactly once. `couple_list`: the row of a cluster t of level l lists in slot j the cluster s = 4 * (t // 4 - 2) + j of level l if s exists, the parents of t and s are near and t and s are not near, else -1. `root_list`: entry [t, s] is s if roots t and s are not near, else -1.
All inputs are finite; a program needn't handle non-finite values.
Results may differ from a plain program's by a relative error of at most 0.0003.
Values sent between devices are 32-bit elements; how exact they have to be, the bound alone decides.
No kernel may reach another device: no remote copies, remote signals or barrier semaphores. Data moves between devices by JAX's collectives and lax.ppermute only.
A program may use at most 128 MiB of HBM per device.

v0:
```python
import math

import jax
import jax.numpy as jnp
from jax import lax
from jax.sharding import PartitionSpec as P

LEAF = 64
LEVELS = 3
REACH = 2
HALO = 11
LEAF_DEV = 64


kernel_band = 0.1
highest = lax.Precision.HIGHEST


def with_halo_2(cells, sides, width):
    for axis, dim in sides:
        count = lax.axis_size(axis)
        ends = count - 1
        head = lax.slice_in_dim(cells, 0, width, axis=dim)
        tail = lax.slice_in_dim(cells, cells.shape[dim] - width, cells.shape[dim], axis=dim)
        cells = jnp.concatenate(
            [
                lax.ppermute(tail, axis, [(i, (i + 1) % count) for i in range(ends)]),
                cells,
                lax.ppermute(head, axis, [((i + 1) % count, i) for i in range(ends)]),
            ],
            axis=dim,
        )
    return cells


def kernel_sq(left_pts, right_pts):
    length = (
        (left_pts[0] - right_pts[0]) ** 2
        + (left_pts[1] - right_pts[1]) ** 2
        + (left_pts[2] - right_pts[2]) ** 2
    )
    return jnp.exp(-length / kernel_band)


def by_blocks(method, inputs, length, stride, out_shape):
    stride = math.gcd(length, stride)

    def advance(step_no, accumulated):
        pieces = [operand for operand in inputs]
        return method(*pieces)

    return lax.fori_loop(0, length // stride, advance, jnp.zeros(out_shape, jnp.float32))


def couple(target_prox, lookup, source_prox, listed):
    usable = listed.T >= 0
    clipped = jnp.where(usable, listed.T, 0)

    def one_block(target_blk, clipped_blk, usable_blk):
        coeff_blk = jnp.take(lookup, clipped_blk, axis=2)
        prox_blk = jnp.take(source_prox, clipped_blk, axis=2)
        kernel = kernel_sq(
            target_blk[:, :, None, None, :], prox_blk[:, None, :, :, :]
        ) * usable_blk.astype(coeff_blk.dtype)
        return jnp.einsum("absn,bksn->akn", kernel, coeff_blk, precision=highest)

    extent = listed.shape[0]
    return by_blocks(
        one_block,
        [target_prox, clipped, usable],
        extent,
        128,
        (lookup.shape[0], lookup.shape[1], extent),
    )


def near_local(targets, lookup, listed, vectors):
    leaves = targets.shape[1]
    total = jnp.zeros((vectors, leaves, targets.shape[2]), jnp.float32)
    for slot_no in range(listed.shape[1]):
        window = lookup[:, slot_no : slot_no + leaves]
        usable = (listed[:, slot_no] >= 0).astype(jnp.float32)
        kernel = (
            kernel_sq(targets[:, :, :, None], window[vectors:, :, None, :]) * usable[:, None, None]
        )
        total = total + jnp.einsum("nij,knj->kni", kernel, window[:vectors], precision=highest)
    return total


def body(points, rhs, leaf_basis, transfer, proxies, near_list, couple_list, root_list):
    device = lax.axis_index("leaf")
    rank_dim = leaf_basis.shape[0]
    vectors = rhs.shape[0]
    leaves = LEAF_DEV
    basis_grid = leaf_basis.reshape(rank_dim, leaves, LEAF)
    coeffs = [None] * (LEVELS + 1)
    coeffs[LEVELS] = jnp.einsum(
        "rnp,knp->rkn", basis_grid, rhs.reshape(vectors, leaves, LEAF), precision=highest
    )
    level_prox = []
    mappings = [None]
    entries = [None]
    for level_no in range(LEVELS + 1):
        extent = 4**level_no
        begin_at = (extent - 1) // 3
        level_prox.append(proxies[:, :, begin_at : begin_at + extent])
        if level_no > 0:
            mappings.append(transfer[:, :, begin_at - 1 : begin_at - 1 + extent])
            entries.append(couple_list[begin_at - 1 : begin_at - 1 + extent])
    for level_no in range(LEVELS, 0, -1):
        merged = jnp.einsum("abn,akn->bkn", mappings[level_no], coeffs[level_no], precision=highest)
        coeffs[level_no - 1] = merged.reshape(rank_dim, vectors, -1, 4).sum(axis=3)
    top_count = 3
    stacked_coeffs = jnp.concatenate([coeffs[level_no] for level_no in range(top_count)], axis=2)
    stacked_prox = jnp.concatenate(level_prox[:top_count], axis=2)
    gathered_coeffs, gathered_prox = (
        lax.all_gather(stacked_coeffs, "leaf", axis=2, tiled=True),
        lax.all_gather(stacked_prox, "leaf", axis=2, tiled=True),
    )
    group = stacked_coeffs.shape[2]
    roots = gathered_coeffs.shape[2] // group
    gathered_coeffs = gathered_coeffs.reshape(rank_dim, vectors, roots, group)
    gathered_prox = gathered_prox.reshape(3, rank_dim, roots, group)
    coupled = []
    for level_no in range(LEVELS + 1):
        extent = 4**level_no
        if level_no < top_count:
            begin_at = (extent - 1) // 3
            lookup = gathered_coeffs[:, :, :, begin_at : begin_at + extent].reshape(
                rank_dim, vectors, roots * extent
            )
            source_prox = gathered_prox[:, :, :, begin_at : begin_at + extent].reshape(
                3, rank_dim, roots * extent
            )
            listed = root_list if level_no == 0 else entries[level_no]
        else:
            joined = jnp.concatenate(
                [
                    coeffs[level_no].reshape(rank_dim * vectors, extent),
                    level_prox[level_no].reshape(3 * rank_dim, extent),
                ],
                axis=0,
            )
            with_rim = with_halo_2(joined, (("leaf", 1),), HALO)
            width_rim = with_rim.shape[1]
            lookup = with_rim[: rank_dim * vectors].reshape(rank_dim, vectors, width_rim)
            source_prox = with_rim[rank_dim * vectors :].reshape(3, rank_dim, width_rim)
            base_index = device * extent - HALO
            listed = jnp.where(entries[level_no] >= 0, entries[level_no] - base_index, -1)
        coupled.append(couple(level_prox[level_no], lookup, source_prox, listed))
    downward = coupled[0]
    for level_no in range(1, LEVELS + 1):
        downward = coupled[level_no] + jnp.einsum(
            "abn,bkn->akn", mappings[level_no], jnp.repeat(downward, 4, axis=2), precision=highest
        )
    joined_pts = jnp.concatenate([rhs, points], axis=0)
    with_halo = with_halo_2(joined_pts, (("leaf", 1),), REACH * LEAF)
    lookup_pts = with_halo.reshape(vectors + 3, leaves + 2 * REACH, LEAF)
    targets = points.reshape(3, leaves, LEAF)
    near_part = near_local(targets, lookup_pts, near_list, vectors)
    far_part = jnp.einsum("rnp,rkn->knp", basis_grid, downward, precision=highest)
    return (near_part + far_part).reshape(vectors, leaves * LEAF)


def solution(mesh):
    in_specs = (
        P(None, "leaf"),
        P(None, "leaf"),
        P(None, "leaf"),
        P(None, None, "leaf"),
        P(None, None, "leaf"),
        P("leaf", None),
        P("leaf", None),
        P("leaf", None),
    )
    out_specs = P(None, "leaf")
    return jax.shard_map(body, mesh=mesh, in_specs=in_specs, out_specs=out_specs, check_vma=False)
```

profile of v0, /device:TPU:0, one launch (start us, length us, event | category | flops | bytes accessed | tf_op | source)
XLA Modules:
  0.0 221.3 jit_solution(3418273684707584734)
XLA Ops:
  6.5 1.3 slice.387
  7.9 2.0 slice.388
  10.3 1.2 reshape.363
  11.5 0.9 copy.165
  12.4 1.7 copy.166
  14.4 3.6 %convolution_bitcast_fusion = f32[32,16,64]{0,1,2:T(8,128)S(1)} fusion(f32[32,64,64]{2,1,0:T(8,128)S(1)} %reshape.364, f32[16,64,64]{2,1,0:T(8,128)} %reshape.363), kind=kOutput, calls=%fused_computation.140 | convolution fusion | flops 25165824 | bytes 917504 | tf_op jit(solution)/shard_map/rnp,knp->rkn/dot_general | solution.py:97
  18.1 1.0 bitcast_reduce_fusion
  19.7 0.7 pad_maximum_fusion.3
  20.9 0.9 slice_maximum_fusion
  21.8 2.4 %collective-permute-start.2 = (f32[608,11]{1,0:T(8,128)}, f32[608,11]{1,0:T(8,128)S(1)}, u32[]{:S(2)}, u32[]{:S(2)}) collective-permute-start(f32[608,11]{1,0:T(8,128)} %get-tuple-element.121), channel_id=1, source_target_pairs={{0,1},{1,2},{2,3},{3,4},{4,5},{5,6},{6,7},{7,8},{8,9},{9,10},{10,1... | collective-permute-start | bytes 80264 | tf_op jit(solution)/shard_map/ppermute | solution.py:27
  24.2 1.3 collective-permute-start.3
  26.2 5.7 %collective-permute-start = (f32[19,128]{1,0:T(8,128)}, f32[19,128]{1,0:T(8,128)}, u32[]{:S(2)}, u32[]{:S(2)}) collective-permute-start(f32[19,128]{1,0:T(8,128)} %get-tuple-element.119), channel_id=1, source_target_pairs={{0,1},{1,2},{2,3},{3,4},{4,5},{5,6},{6,7},{7,8},{8,9},{9,10},{10,1... | collective-permute-start | bytes 29192 | tf_op jit(solution)/shard_map/ppermute | solution.py:27
  31.9 1.3 collective-permute-start.1
  33.9 0.7 fusion.264
  34.7 50.4 %all_gather.7 = f32[3,32,672]{1,0,2:T(4,128)S(1)} all-gather(f32[3,32,21]{1,0,2:T(4,128)S(1)} %copy.169), channel_id=1, replica_groups=mesh['leaf'=32] {'leaf'}, dimensions={2}, use_global_device_ids=true | all-gather | bytes 266112 | tf_op jit(solution)/shard_map/all_gather | solution.py:118
  85.7 0.7 slice_reduce_fusion.2
  87.3 0.7 slice_bitcast_fusion.28
  88.0 0.7 slice_bitcast_fusion.31
  89.8 0.7 gather_fusion.5
  93.2 2.2 gather_fusion.3
  95.7 0.8 slice_bitcast_fusion.6
  101.2 0.7 copy.121
  101.9 0.7 copy.125
  102.6 0.7 copy.127
  103.5 0.8 pad_maximum_fusion
  104.8 6.1 %fusion.87 = f32[64,16,64]{2,1,0:T(8,128)S(1)} fusion(f32[64]{0:T(128)S(1)} %get-tuple-element.145, f32[64,64]{1,0:T(8,128)S(1)} %get-tuple-element.100, f32[64,64]{1,0:T(8,128)S(1)} %get-tuple-element.101, f32[64,64]{1,0:T(8,128)S(1)} %get-tuple-element.102, f32[64,64]{1,0:T(8,128)S(1)} %sub.523, f32[64,64]{1,0:T(8,128)S(1)} %sub.518, ...), kind=kOutput, calls=%fused_computation.95 | convolution fusion | flops 53215232 | bytes 622848 | tf_op jit(solution)/shard_map/nij,knj->kni/dot_general | solution.py:86
  110.9 6.1 %fusion.74 = f32[64,16,64]{2,1,0:T(8,128)S(1)} fusion(f32[64]{0:T(128)S(1)} %get-tuple-element.144, f32[64,64]{1,0:T(8,128)S(1)} %get-tuple-element.89, f32[64,64]{1,0:T(8,128)S(1)} %get-tuple-element.90, f32[64,64]{1,0:T(8,128)S(1)} %get-tuple-element.98, f32[64,64]{1,0:T(8,128)S(1)} %sub.523, f32[64,64]{1,0:T(8,128)S(1)} %sub.518, ...), kind=kOutput, calls=%fused_computation.82 | convolution fusion | flops 53215232 | bytes 622848 | tf_op jit(solution)/shard_map/nij,knj->kni/dot_general | solution.py:86
  117.0 6.1 %fusion.48 = f32[64,16,64]{2,1,0:T(8,128)S(1)} fusion(f32[64]{0:T(128)S(1)} %get-tuple-element.147, f32[64,64]{1,0:T(8,128)S(1)} %get-tuple-element.103, f32[64,64]{1,0:T(8,128)S(1)} %get-tuple-element.99, f32[64,64]{1,0:T(8,128)S(1)} %get-tuple-element.88, f32[64,64]{1,0:T(8,128)S(1)} %sub.523, f32[64,64]{1,0:T(8,128)S(1)} %sub.518, ...), kind=kOutput, calls=%fused_computation.56 | convolution fusion | flops 53215232 | bytes 622848 | tf_op jit(solution)/shard_map/nij,knj->kni/dot_general | solution.py:86
  123.0 6.1 %fusion.138 = f32[64,16,64]{2,1,0:T(8,128)S(1)} fusion(f32[64,16,64]{2,1,0:T(8,128)S(1)} %fusion.74, f32[64,16,64]{2,1,0:T(8,128)S(1)} %fusion.87, f32[64]{0:T(128)S(1)} %get-tuple-element.146, f32[64,64]{1,0:T(8,128)S(1)} %get-tuple-element.104, f32[64,64]{1,0:T(8,128)S(1)} %sub.523, f32[64,64]{1,0:T(8,128)S(1)} %get-tuple-element.112, ...), kind=kOutput, calls=%fused_computation.143 | convolution fusion | flops 53346304 | bytes 1147136 | tf_op jit(solution)/shard_map/nij,knj->kni/dot_general | solution.py:86
  129.1 6.0 %fusion.144 = f32[64,16,64]{2,1,0:T(8,128)} fusion(f32[64,16,64]{2,1,0:T(8,128)S(1)} %fusion.48, f32[64,16,64]{2,1,0:T(8,128)S(1)} %fusion.138, f32[64]{0:T(128)S(1)} %get-tuple-element.143, f32[64,64]{1,0:T(8,128)S(1)} %get-tuple-element.86, f32[64,64]{1,0:T(8,128)S(1)} %get-tuple-element.87, f32[64,64]{1,0:T(8,128)S(1)} %get-tuple-element.85, ...), kind=kOutput, calls=%fused_computation.145 | convolution fusion | flops 53346304 | bytes 1147136 | tf_op jit(solution)/shard_map/nij,knj->kni/dot_general | solution.py:86
  136.1 4.3 %gather_fusion.1 = f32[1280,3,32]{2,1,0:T(4,128)S(1)} fusion(f32[3,32,86]{1,0,2:T(4,128)S(1)} %copy.122, s32[2048]{0:T(1024)S(1)} %pad_clamp_fusion), kind=kCustom, calls=%fused_computation.1 | custom fusion | bytes 988160 | tf_op jit(solution)/shard_map/while/body/eval_jaxpr/jit(_take)/gather | solution.py:61
  140.4 2.6 %copy.154 = f32[20,64,3,32]{1,0,3,2:T(8,128)} copy(f32[20,64,3,32]{3,2,1,0:T(4,128)S(1)} %bitcast.205) | data formatting | bytes 983040 | tf_op jit(solution)/shard_map/while/body/eval_jaxpr/jit(_take)/gather | solution.py:61
  143.0 1.4 select_bitcast_fusion
  144.7 1.1 copy.126
  145.8 1.1 copy.128
  147.7 5.5 %gather_fusion = f32[1280,32,16]{1,2,0:T(8,128)} fusion(f32[32,16,86]{0,1,2:T(8,128)S(1)} %copy.120, s32[2048]{0:T(1024)S(1)} %pad_clamp_fusion), kind=kCustom, calls=%fused_computation | custom fusion | bytes 5248000 | tf_op jit(solution)/shard_map/while/body/eval_jaxpr/jit(_take)/gather | solution.py:60
  153.2 31.3 %fusion.130 = f32[64,16,32]{2,1,0:T(8,128)} fusion(f32[20,64]{1,0:T(8,128)S(1)} %copy-done.44, f32[32,20,64]{0,2,1:T(8,128)S(1)} %copy-done.15, f32[32,64]{0,1:T(8,128)S(1)} %copy-done.39, f32[32,20,64]{0,2,1:T(8,128)S(1)} %copy-done.14, f32[32,64]{0,1:T(8,128)S(1)} %copy-done.38, f32[32,20,64]{0,2,1:T(8,128)S(1)} %copy.124, f32[32,64]{0,1:T(8,128)S(1)} %copy-done.37, ...), kind=kOutput, calls=%fused_computation.141 | convolution fusion | flops 266731520 | bytes 3275008 | tf_op jit(solution)/shard_map/while/body/eval_jaxpr/absn,bksn->akn/dot_general | solution.py:65
  184.5 1.3 slice.465
  185.9 1.0 slice_bitcast_fusion.3
  186.8 4.6 %slice.460 = f32[32,16,32,16]{0,1,3,2:T(8,128)} slice(f32[32,16,32,21]{0,1,3,2:T(8,128)} %bitcast.208), slice={[0:32], [0:16], [0:32], [5:21]} | slice | bytes 2097152 | tf_op jit(solution)/shard_map/slice | solution.py:129
  192.1 1.4 gather_fusion.6
  193.5 3.0 %gather_fusion.2 = f32[320,32,16]{1,2,0:T(8,128)S(1)} fusion(f32[32,16,512]{0,1,2:T(8,128)} %bitcast.203, s32[1024]{0:T(1024)S(1)} %get-tuple-element.151), kind=kCustom, calls=%fused_computation.2 | custom fusion | bytes 1312000 | tf_op jit(solution)/shard_map/while/body/eval_jaxpr/jit(_take)/gather | solution.py:60
  196.7 3.1 %fusion.153 = f32[4,16,32]{2,1,0:T(8,128)S(1)} fusion(f32[20,4,32,16]{2,3,1,0:T(8,128)S(1)} %bitcast.201, f32[20,4]{1,0:T(8,128)} %get-tuple-element.139, f32[32,20,4]{0,2,1:T(4,128)} %get-tuple-element.124, f32[32,4]{0,1:T(4,128)} %bitcast.234, f32[32,20,4]{0,2,1:T(4,128)} %get-tuple-element.125, f32[32,4]{0,1:T(4,128)} %bitcast.233, ...), kind=kOutput, calls=%fused_computation.150 | convolution fusion | flops 16670720 | bytes 204688 | tf_op jit(solution)/shard_map/while/body/eval_jaxpr/absn,bksn->akn/dot_general | solution.py:65
  200.0 0.8 convolution_bitcast_fusion.1
  201.1 8.3 %fusion.148 = f32[16,16,32]{2,1,0:T(8,128)S(1)} fusion(f32[20,16]{1,0:T(8,128)S(1)} %copy-done.43, f32[32,20,16]{0,2,1:T(8,128)S(1)} %copy-done.25, f32[32,16]{0,1:T(8,128)S(1)} %copy-done.47, f32[32,20,16]{0,2,1:T(8,128)S(1)} %copy-done.26, f32[32,16]{0,1:T(8,128)S(1)} %copy-done.46, f32[32,20,16]{0,2,1:T(8,128)S(1)} %copy-done.24, ...), kind=kOutput, calls=%fused_computation.149 | convolution fusion | flops 66682880 | bytes 818752 | tf_op jit(solution)/shard_map/while/body/eval_jaxpr/absn,bksn->akn/dot_general | solution.py:65
  210.0 1.7 fusion.129
  211.8 1.6 fusion.128
  213.6 0.9 reshape.382
  (186 shorter events, 17.7 us)
Async XLA Ops:
  6.5 3.4 %copy-start.18 = (f32[32,4096]{1,0:T(8,128)S(1)}, f32[32,4096]{1,0:T(8,128)}, u32[]{:S(2)}) copy-start(f32[32,4096]{1,0:T(8,128)} %param.10) | copy-start | bytes 1572868
  6.5 3.8 %copy-start.10 = (f32[16,4096]{1,0:T(8,128)S(1)}, f32[16,4096]{1,0:T(8,128)}, u32[]{:S(2)}) copy-start(f32[16,4096]{1,0:T(8,128)} %param.9) | copy-start | bytes 786436
  6.5 178.0 %all-gather.2.cloned.1.call-start = ((), (), s32[]{:S(2)}) async-start(), calls=%async_computation | async-start | bytes 5677056 | tf_op jit(solution)/shard_map/all_gather | solution.py:117
  9.9 4.2 %copy-start.4 = (f32[32,32,84]{2,1,0:T(8,128)S(1)}, f32[32,32,84]{2,1,0:T(8,128)}, u32[]{:S(2)}) copy-start(f32[32,32,84]{2,1,0:T(8,128)} %param.11) | copy-start | bytes 1032196
  10.3 7.7 %copy-start = (f32[32,64,64]{2,1,0:T(8,128)}, f32[32,64,64]{2,1,0:T(8,128)S(1)}, u32[]{:S(2)}) copy-start(f32[32,64,64]{2,1,0:T(8,128)S(1)} %reshape.364) | copy-start | bytes 1572868
  12.4 6.7 %copy-start.2 = (f32[32,32,64]{1,0,2:T(8,128)}, f32[32,32,64]{1,0,2:T(8,128)S(1)}, u32[]{:S(2)}) copy-start(f32[32,32,64]{1,0,2:T(8,128)S(1)} %copy.165) | copy-start | bytes 786436
  14.4 5.1 %copy-start.16 = (f32[32,32,4]{1,0,2:T(8,128)}, f32[32,32,4]{1,0,2:T(8,128)S(1)}, u32[]{:S(2)}) copy-start(f32[32,32,4]{1,0,2:T(8,128)S(1)} %copy.167) | copy-start | bytes 49156
  19.1 6.4 %copy-start.11 = (f32[16,4096]{1,0:T(8,128)S(1)}, f32[16,4096]{1,0:T(8,128)}, u32[]{:S(2)}) copy-start(f32[16,4096]{1,0:T(8,128)} %param.9) | copy-start | bytes 786436
  19.1 6.4 %copy-start.23 = (f32[3,4096]{1,0:T(4,128)S(1)}, f32[3,4096]{1,0:T(4,128)}, u32[]{:S(2)}) copy-start(f32[3,4096]{1,0:T(4,128)} %param.8) | copy-start | bytes 147460
  19.1 14.1 %copy-start.21 = (s32[84,20]{0,1:T(8,128)S(1)}, s32[84,20]{0,1:T(8,128)}, u32[]{:S(2)}) copy-start(s32[84,20]{0,1:T(8,128)} %param.14) | copy-start | bytes 20164
  20.8 64.3 %copy-start.55 = (s32[1,32]{1,0:T(1,128)S(1)}, s32[1,32]{1,0:T(1,128)}, u32[]{:S(2)}) copy-start(s32[1,32]{1,0:T(1,128)} %param.15) | copy-start | bytes 388
  20.9 114.2 %copy-start.12 = (f32[3,32,64]{2,1,0:T(8,128)}, f32[3,32,64]{2,1,0:T(8,128)S(1)}, u32[]{:S(2)}) copy-start(f32[3,32,64]{2,1,0:T(8,128)S(1)} %slice.375) | copy-start | bytes 73732
  21.8 113.3 %collective-permute-start.2 = (f32[608,11]{1,0:T(8,128)}, f32[608,11]{1,0:T(8,128)S(1)}, u32[]{:S(2)}, u32[]{:S(2)}) collective-permute-start(f32[608,11]{1,0:T(8,128)} %get-tuple-element.121), channel_id=1, source_target_pairs={{0,1},{1,2},{2,3},{3,4},{4,5},{5,6},{6,7},{7,8},{8,9},{9,10},{10,1... | collective-permute-start | bytes 80264 | tf_op jit(solution)/shard_map/ppermute | solution.py:27
  24.2 110.9 %collective-permute-start.3 = (f32[608,11]{1,0:T(8,128)}, f32[608,11]{1,0:T(8,128)S(1)}, u32[]{:S(2)}, u32[]{:S(2)}) collective-permute-start(f32[608,11]{1,0:T(8,128)} %get-tuple-element.122), channel_id=1, source_target_pairs={{1,0},{2,1},{3,2},{4,3},{5,4},{6,5},{7,6},{8,7},{9,8},{10,9},{11,1... | collective-permute-start | bytes 80264 | tf_op jit(solution)/shard_map/ppermute | solution.py:29
  26.2 77.3 %collective-permute-start = (f32[19,128]{1,0:T(8,128)}, f32[19,128]{1,0:T(8,128)}, u32[]{:S(2)}, u32[]{:S(2)}) collective-permute-start(f32[19,128]{1,0:T(8,128)} %get-tuple-element.119), channel_id=1, source_target_pairs={{0,1},{1,2},{2,3},{3,4},{4,5},{5,6},{6,7},{7,8},{8,9},{9,10},{10,1... | collective-permute-start | bytes 29192 | tf_op jit(solution)/shard_map/ppermute | solution.py:27
  31.9 71.6 %collective-permute-start.1 = (f32[19,128]{1,0:T(8,128)}, f32[19,128]{1,0:T(8,128)}, u32[]{:S(2)}, u32[]{:S(2)}) collective-permute-start(f32[19,128]{1,0:T(8,128)} %get-tuple-element.120), channel_id=1, source_target_pairs={{1,0},{2,1},{3,2},{4,3},{5,4},{6,5},{7,6},{8,7},{9,8},{10,9},{11,1... | collective-permute-start | bytes 29192 | tf_op jit(solution)/shard_map/ppermute | solution.py:29
  85.7 6.2 %copy-start.50 = (pred[32]{0:T(512)(128)(4,1)}, pred[32]{0:T(512)(128)(4,1)S(1)}, u32[]{:S(2)}) copy-start(pred[32]{0:T(512)(128)(4,1)S(1)} %get-tuple-element.148) | copy-start | bytes 100
  91.2 4.2 %copy-start.48 = (s32[1024]{0:T(1024)}, s32[1024]{0:T(1024)S(1)}, u32[]{:S(2)}) copy-start(s32[1024]{0:T(1024)S(1)} %pad_clamp_fusion.1) | copy-start | bytes 12292
  95.5 3.8 %copy-start.36 = (f32[32,16]{1,0:T(8,128)S(1)}, f32[32,16]{1,0:T(8,128)}, u32[]{:S(2)}) copy-start(f32[32,16]{1,0:T(8,128)} %get-tuple-element.132) | copy-start | bytes 6148
  95.5 4.4 %copy-start.35 = (f32[32,16]{1,0:T(8,128)S(1)}, f32[32,16]{1,0:T(8,128)}, u32[]{:S(2)}) copy-start(f32[32,16]{1,0:T(8,128)} %get-tuple-element.134) | copy-start | bytes 6148
  95.5 5.1 %copy-start.34 = (f32[32,16]{1,0:T(8,128)S(1)}, f32[32,16]{1,0:T(8,128)}, u32[]{:S(2)}) copy-start(f32[32,16]{1,0:T(8,128)} %get-tuple-element.133) | copy-start | bytes 6148
  95.5 5.7 %copy-start.30 = (f32[32,64]{1,0:T(8,128)S(1)}, f32[32,64]{1,0:T(8,128)}, u32[]{:S(2)}) copy-start(f32[32,64]{1,0:T(8,128)} %get-tuple-element.135) | copy-start | bytes 24580
  95.5 6.4 %copy-start.29 = (f32[32,64]{1,0:T(8,128)S(1)}, f32[32,64]{1,0:T(8,128)}, u32[]{:S(2)}) copy-start(f32[32,64]{1,0:T(8,128)} %get-tuple-element.137) | copy-start | bytes 24580
  95.5 7.1 %copy-start.28 = (f32[32,64]{1,0:T(8,128)S(1)}, f32[32,64]{1,0:T(8,128)}, u32[]{:S(2)}) copy-start(f32[32,64]{1,0:T(8,128)} %get-tuple-element.136) | copy-start | bytes 24580
  95.5 7.8 %copy-start.27 = (f32[4096]{0:T(1024)S(1)}, f32[4096]{0:T(1024)}, u32[]{:S(2)}) copy-start(f32[4096]{0:T(1024)} %get-tuple-element.48) | copy-start | bytes 49156
  147.6 5.6 %copy-start.14 = (f32[32,20,64]{0,2,1:T(8,128)S(1)}, f32[32,20,64]{0,2,1:T(8,128)}, u32[]{:S(2)}) copy-start(f32[32,20,64]{0,2,1:T(8,128)} %copy.126) | copy-start | bytes 491524
  147.6 5.6 %copy-start.15 = (f32[32,20,64]{0,2,1:T(8,128)S(1)}, f32[32,20,64]{0,2,1:T(8,128)}, u32[]{:S(2)}) copy-start(f32[32,20,64]{0,2,1:T(8,128)} %copy.128) | copy-start | bytes 491524
  147.6 5.6 %copy-start.37 = (f32[32,64]{0,1:T(8,128)S(1)}, f32[32,64]{0,1:T(8,128)}, u32[]{:S(2)}) copy-start(f32[32,64]{0,1:T(8,128)} %copy.121) | copy-start | bytes 24580
  147.6 5.6 %copy-start.38 = (f32[32,64]{0,1:T(8,128)S(1)}, f32[32,64]{0,1:T(8,128)}, u32[]{:S(2)}) copy-start(f32[32,64]{0,1:T(8,128)} %copy.125) | copy-start | bytes 24580
  147.7 5.6 %copy-start.39 = (f32[32,64]{0,1:T(8,128)S(1)}, f32[32,64]{0,1:T(8,128)}, u32[]{:S(2)}) copy-start(f32[32,64]{0,1:T(8,128)} %copy.127) | copy-start | bytes 24580
  147.7 5.6 %copy-start.44 = (f32[20,64]{1,0:T(8,128)S(1)}, f32[20,64]{1,0:T(8,128)}, u32[]{:S(2)}) copy-start(f32[20,64]{1,0:T(8,128)} %get-tuple-element.142) | copy-start | bytes 15364
  196.6 3.3 %copy-start.22 = (f32[32,32,16]{1,2,0:T(8,128)S(1)}, f32[32,32,16]{1,2,0:T(8,128)}, u32[]{:S(2)}) copy-start(f32[32,32,16]{1,2,0:T(8,128)} %gather_fusion.6) | copy-start | bytes 196612
  196.6 3.3 %copy-start.40 = (f32[1,32,32,1]{1,0,2,3:T(1,128)S(1)}, f32[1,32,32,1]{1,0,2,3:T(1,128)}, u32[]{:S(2)}) copy-start(f32[1,32,32,1]{1,0,2,3:T(1,128)} %get-tuple-element.126) | copy-start | bytes 12292
  196.6 3.3 %copy-start.41 = (f32[1,32,32,1]{1,0,2,3:T(1,128)S(1)}, f32[1,32,32,1]{1,0,2,3:T(1,128)}, u32[]{:S(2)}) copy-start(f32[1,32,32,1]{1,0,2,3:T(1,128)} %get-tuple-element.127) | copy-start | bytes 12292
  196.6 3.3 %copy-start.42 = (f32[1,32,32,1]{1,0,2,3:T(1,128)S(1)}, f32[1,32,32,1]{1,0,2,3:T(1,128)}, u32[]{:S(2)}) copy-start(f32[1,32,32,1]{1,0,2,3:T(1,128)} %get-tuple-element.128) | copy-start | bytes 12292
  196.6 3.3 %copy-start.51 = (pred[32]{0:T(512)(128)(4,1)S(1)}, pred[32]{0:T(512)(128)(4,1)}, u32[]{:S(2)}) copy-start(pred[32]{0:T(512)(128)(4,1)} %copy-done.50) | copy-start | bytes 100
  196.6 3.3 %copy-start.52 = (f32[32]{0:T(128)S(1)}, f32[32]{0:T(128)}, u32[]{:S(2)}) copy-start(f32[32]{0:T(128)} %get-tuple-element.58) | copy-start | bytes 388
  196.6 3.3 %copy-start.53 = (f32[32]{0:T(128)S(1)}, f32[32]{0:T(128)}, u32[]{:S(2)}) copy-start(f32[32]{0:T(128)} %get-tuple-element.59) | copy-start | bytes 388
  196.6 4.1 %copy-start.17 = (f32[32,32,4]{1,0,2:T(8,128)S(1)}, f32[32,32,4]{1,0,2:T(8,128)}, u32[]{:S(2)}) copy-start(f32[32,32,4]{1,0,2:T(8,128)} %copy-done.16) | copy-start | bytes 49156
  196.7 4.4 %copy-start.24 = (f32[32,20,16]{0,2,1:T(8,128)S(1)}, f32[32,20,16]{0,2,1:T(8,128)}, u32[]{:S(2)}) copy-start(f32[32,20,16]{0,2,1:T(8,128)} %get-tuple-element.116) | copy-start | bytes 122884
  196.7 4.4 %copy-start.25 = (f32[32,20,16]{0,2,1:T(8,128)S(1)}, f32[32,20,16]{0,2,1:T(8,128)}, u32[]{:S(2)}) copy-start(f32[32,20,16]{0,2,1:T(8,128)} %get-tuple-element.117) | copy-start | bytes 122884
  196.7 4.4 %copy-start.26 = (f32[32,20,16]{0,2,1:T(8,128)S(1)}, f32[32,20,16]{0,2,1:T(8,128)}, u32[]{:S(2)}) copy-start(f32[32,20,16]{0,2,1:T(8,128)} %get-tuple-element.118) | copy-start | bytes 122884
  196.7 4.4 %copy-start.43 = (f32[20,16]{1,0:T(8,128)S(1)}, f32[20,16]{1,0:T(8,128)}, u32[]{:S(2)}) copy-start(f32[20,16]{1,0:T(8,128)} %get-tuple-element.141) | copy-start | bytes 3844
  196.7 4.4 %copy-start.45 = (f32[32,16]{0,1:T(8,128)S(1)}, f32[32,16]{0,1:T(8,128)}, u32[]{:S(2)}) copy-start(f32[32,16]{0,1:T(8,128)} %copy.135) | copy-start | bytes 6148
  196.7 4.4 %copy-start.46 = (f32[32,16]{0,1:T(8,128)S(1)}, f32[32,16]{0,1:T(8,128)}, u32[]{:S(2)}) copy-start(f32[32,16]{0,1:T(8,128)} %copy.141) | copy-start | bytes 6148
  196.7 4.4 %copy-start.47 = (f32[32,16]{0,1:T(8,128)S(1)}, f32[32,16]{0,1:T(8,128)}, u32[]{:S(2)}) copy-start(f32[32,16]{0,1:T(8,128)} %copy.142) | copy-start | bytes 6148
  201.1 8.9 %copy-start.3 = (f32[32,32,64]{1,0,2:T(8,128)S(1)}, f32[32,32,64]{1,0,2:T(8,128)}, u32[]{:S(2)}) copy-start(f32[32,32,64]{1,0,2:T(8,128)} %copy-done.2) | copy-start | bytes 786436
  201.1 8.9 %copy-start.20 = (f32[64,16,32]{2,1,0:T(8,128)S(1)}, f32[64,16,32]{2,1,0:T(8,128)}, u32[]{:S(2)}) copy-start(f32[64,16,32]{2,1,0:T(8,128)} %fusion.130) | copy-start | bytes 393220
  (14 other events, 32.4 us)
Sparse Core Ops, SparseCore 0:
  20.6 72.6 all-gather.1
where the time goes:
time: 222 us; the launch traced here: 221 us
  matrix products  83.1 us (37%)
  local copies, waits for them, and re-layouts  55.7 us (25%)
  blocking collectives  50.4 us (23%)
  between operations  14.5 us (7%)
  starting transfers between devices  10.7 us (5%)
  other arithmetic  6.98 us (3%)
    all_gather x1, blocking collectives, body(): lax.all_gather(stacked_prox, 'leaf', axis=2, tiled=True)  50.4 us
    dot_general x4, matrix products, one_block(): return jnp.einsum('absn,bksn->akn', kernel, coeff_blk, precision=highest)  43.6 us
    dot_general x5, matrix products, near_local(): jnp.einsum('nij,knj->kni', kernel, window[:vectors], precision=highest)  30.2 us
    gather x4, local copies, waits for them, and re-layouts, one_block(): coeff_blk = jnp.take(lookup, clipped_blk, axis=2)  10.6 us
    gather x7, local copies, waits for them, and re-layouts, one_block(): prox_blk = jnp.take(source_prox, clipped_blk, axis=2)  10.4 us
    ppermute x2, starting transfers between devices, with_halo_2(): lax.ppermute(tail, axis, [(i, (i + 1) % count) for i in range(ends)])  8.1 us
    slice x2, local copies, waits for them, and re-layouts, body(): gathered_coeffs[:, :, :, begin_at:begin_at + extent]  5.94 us
    sub x10, local copies, waits for them, and re-layouts, kernel_sq(): left_pts[0] - right_pts[0]  4.64 us
  transfers between devices with their start and end apart: 5, of which 0 were waited for; matrix products, arithmetic and copies ran while one was open for 46% of the time, Pallas kernels for 0%

commit v1 on v0

v1 whole, which is shorter than its diff:
```python
import math

import jax
import jax.numpy as jnp
from jax import lax
from jax.experimental import pallas as pl
from jax.experimental.pallas import tpu as pltpu
from jax.sharding import PartitionSpec as P

LEVELS = 3
REACH = 2
FAN = 4
LANES = 128
ROWS = 24
FEATS = 32
SCALE = 10.0 * math.log2(math.e)
F32 = jnp.float32
BF16 = jnp.bfloat16

NN = (((1,), (0,)), ((), ()))
NT = (((1,), (1,)), ((), ()))
TN = (((0,), (0,)), ((), ()))


def dot(lhs, rhs, dims=NN):
    return lax.dot_general(lhs, rhs, dims, preferred_element_type=F32)


def split2(value):
    high = value.astype(BF16)
    low = (value - high.astype(F32)).astype(BF16)
    return high, low


def split3(value):
    high = value.astype(BF16).astype(F32)
    rest = value - high
    mid = rest.astype(BF16).astype(F32)
    return high, mid, rest - mid


def stack2(value):
    high, low = split2(value)
    return high, jnp.concatenate([high, low], axis=0)


def dot2(lhs, rhs, dims=NN):
    high, both = stack2(lhs)
    rhs_high, rhs_low = split2(rhs)
    rows = lhs.shape[0]
    wide = dot(both, rhs_high, dims)
    return wide[:rows] + wide[rows:] + dot(high, rhs_low, dims)


def iota(shape, axis):
    return lax.broadcasted_iota(jnp.int32, shape, axis)


def spread(clusters, width, begin, size):
    shape = (clusters, width)
    return (iota(shape, 0) == begin + iota(shape, 1) // size).astype(BF16)


def block_rows(basis, offset, leaf):
    part = basis[:, pl.ds(offset, FAN * leaf)]
    rank = part.shape[0]
    tiled = jnp.concatenate([part] * FAN, axis=0)
    keep = iota(tiled.shape, 0) // rank == iota(tiled.shape, 1) // leaf
    return jnp.where(keep, tiled, 0.0)


def upward_kernel(
    rhs, points, basis, transfer, prox, c3, c2, c1, tile0, right, left, *, leaf, rank, starts
):
    vectors = rhs.shape[0]
    span = FAN * leaf
    group = FAN * rank
    outs = {1: c1, 2: c2, 3: c3}
    for g in range(rhs.shape[1] // span):
        big = block_rows(basis, g * span, leaf)
        c3[:vectors, g * group : (g + 1) * group] = dot2(
            rhs[:, g * span : (g + 1) * span], big, NT
        )
    keep = None
    for level in range(LEVELS, 0, -1):
        source = outs[level]
        count = FAN ** (level - 1)
        base = (starts[level] - 1) * rank
        per = min(FAN, count)
        for h in range(count // per):
            width = per * group
            begin = h * width
            weights = transfer[base + begin : base + begin + width, :]
            keep = iota(weights.shape, 0) // group == iota(weights.shape, 1) // rank
            weights = jnp.where(keep, weights, 0.0)
            merged = dot2(source[:vectors, begin : begin + width], weights)
            if level > 1:
                outs[level - 1][:vectors, h * group : (h + 1) * group] = merged
            else:
                root = merged
    coords = prox.shape[0] // rank
    parts = jnp.concatenate(split3(prox[...]), axis=0).astype(BF16)
    clusters = prox.shape[1]
    for level in range(LEVELS + 1):
        total = max(FAN**level * rank, LANES)
        step = min(total, 512)
        for begin in range(0, total, step):
            cols = spread(clusters, step, starts[level] + begin // rank, rank)
            if level == 0:
                cols = jnp.where(iota(cols.shape, 1) < rank, cols, jnp.zeros_like(cols))
            rows = dot(parts, cols)
            n = coords * rank
            rows = rows[:n] + rows[n : 2 * n] + rows[2 * n :]
            rows = jnp.where(iota(rows.shape, 0) % rank == iota(rows.shape, 1) % rank, rows, 0.0)
            for c in range(coords):
                line = jnp.sum(rows[c * rank : (c + 1) * rank], axis=0, keepdims=True)
                if level == 0:
                    tile0[c : c + 1, :] = line
                else:
                    outs[level][vectors + c : vectors + c + 1, begin : begin + step] = line
    lane = iota((8, LANES), 1)
    for c in range(coords, 8):
        tile0[c : c + 1, :] = jnp.zeros((1, LANES), F32)
    prox_tile = pltpu.roll(tile0[...], 2 * rank, 1)
    lower = jnp.where(lane < rank, root[:8], 0.0)
    upper = pltpu.roll(jnp.where(lane < rank, root[8:16], 0.0), rank, 1)
    tile0[...] = lower + upper + prox_tile
    for level in (1, 2, 3):
        pad = outs[level]
        pad[vectors + coords :, :] = jnp.zeros(
            (ROWS - vectors - coords, pad.shape[1]), F32
        )
    rim = 2 * group
    for send, tail in ((right, True), (left, False)):
        at = 0
        for ref, width in ((c3, rim), (c2, rim), (c1, group)):
            begin = ref.shape[1] - width if tail else 0
            send[:, at : at + width] = ref[:, begin : begin + width]
            at += width
        begin = points.shape[1] - REACH * leaf if tail else 0
        send[:vectors, at:] = rhs[:, begin : begin + REACH * leaf]
        send[vectors : vectors + coords, at:] = points[:, begin : begin + REACH * leaf]
        send[vectors + coords :, at:] = jnp.zeros((ROWS - vectors - coords, REACH * leaf), F32)


def features(position, feats):
    centred = position - 0.5
    high, mid, low = split3(centred)
    wide = centred * (2.0 * SCALE)
    w_high, w_mid, w_low = split3(wide)
    norm = -SCALE * jnp.sum(centred * centred, axis=0, keepdims=True)
    n_parts = split3(norm)
    n = position.shape[1]
    for row, part in enumerate((high, high, high, mid, mid, low)):
        feats[0, 3 * row : 3 * row + 3, :n] = part
    for row, part in enumerate((w_high, w_mid, w_low, w_high, w_mid, w_high)):
        feats[1, 3 * row : 3 * row + 3, :n] = part
    one = jnp.ones((3, n), F32)
    feats[0, 21:24, :n] = one
    feats[1, 18:21, :n] = one
    for row, part in enumerate(n_parts):
        feats[0, 18 + row : 19 + row, :n] = part
        feats[1, 21 + row : 22 + row, :n] = part
    zero = jnp.zeros((FEATS - 24, n), F32)
    feats[0, 24:, :n] = zero
    feats[1, 24:, :n] = zero


def to_rows(feats, rows, begin, n):
    for at in range(0, n, LANES):
        rows[begin + at : begin + at + LANES, :] = jnp.transpose(
            feats[0, :, at : at + LANES]
        ).astype(BF16)


def apply_kernel(kernel, both, vectors):
    high, low = split2(kernel)
    wide = dot(both, high)
    return wide[:vectors] + wide[vectors:] + dot(both[:vectors], low)


def final_kernel(
    device, rhs, points, basis, transfer, near, couple, roots, c3, c2, c1, tile0, gathered,
    from_left, from_right, second_left, second_right, out,
    feats, src, tgt, coef, near_mask, far_mask, field, field2,
    *, leaf, rank, starts, xor,
):
    vectors = rhs.shape[0]
    coords = points.shape[0]
    group = FAN * rank
    rim = 2 * group
    n_points = rhs.shape[1]
    n_leaves = n_points // leaf
    top = vectors + coords

    listed = (near[...] >= 0).astype(F32).astype(BF16)
    near_mask[...] = jnp.zeros(near_mask.shape, F32)
    for at in range(0, n_points, 1024):
        cols = spread(n_leaves, 1024, at // leaf, leaf)
        rows = dot(listed, cols, TN)
        odd = (iota(rows.shape, 1) // leaf) % 2 == 1
        slots = rows.shape[0]
        near_mask[0:slots, at : at + 1024] = jnp.where(odd, 0.0, rows)
        near_mask[1 : slots + 1, at : at + 1024] += jnp.where(odd, rows, 0.0)
    listed = (couple[...] >= 0).astype(F32).astype(BF16)
    n_far = couple.shape[0] * rank
    for at in range(0, n_far, 384):
        cols = spread(couple.shape[0], 384, at // rank, rank)
        far_mask[0 : couple.shape[1], at : at + 384] = dot(listed, cols, TN)

    halo = REACH * leaf
    last = from_left.shape[1] - halo
    for begin, ref, at, n in (
        (0, from_left, last, halo),
        (halo + n_points, from_right, last, halo),
    ):
        features(ref[vectors:top, at : at + n], feats)
        to_rows(feats, src, begin, n)
        coef[:, begin : begin + n] = stack2(ref[:vectors, at : at + n])[1]
    features(points[...], feats)
    to_rows(feats, src, halo, n_points)
    tgt[:, :n_points] = feats[1, :, :n_points].astype(BF16)
    coef[:, halo : halo + n_points] = stack2(rhs[...])[1]

    def near_group(g, carry):
        begin = pl.multiple_of(g * halo, LANES)
        kernel = jnp.exp2(dot(src[pl.ds(begin, 3 * halo), :], tgt[:, pl.ds(begin, halo)]))
        mask = near_mask[:, pl.ds(begin, halo)]
        kernel = jnp.concatenate(
            [kernel[leaf * s : leaf * (s + 1)] * mask[s : s + 1] for s in range(6)], axis=0
        )
        out[:, pl.ds(begin, halo)] = apply_kernel(
            kernel, coef[:, pl.ds(begin, 3 * halo)], vectors
        )
        return carry

    lax.fori_loop(0, n_points // halo, near_group, 0, unroll=4)

    n_roots = roots.shape[1]
    n_all = n_roots * rank
    lane = iota((8, LANES), 1) // rank
    for at in range(0, n_roots, FAN):
        low = jnp.zeros((8, LANES), F32)
        up = low
        place = low
        for j in range(FAN):
            tile = gathered[at + j]
            here = lane == j
            low = jnp.where(here, pltpu.roll(tile, j * rank, 1) if j else tile, low)
            up = jnp.where(here, pltpu.roll(tile, ((j - 1) % FAN) * rank, 1) if j != 1 else tile, up)
            place = jnp.where(
                here, pltpu.roll(tile, ((j - 2) % FAN) * rank, 1) if j != 2 else tile, place
            )
        lanes = slice(at * rank, at * rank + LANES)
        field[0:8, lanes] = low
        field[8:16, lanes] = up
        field[16:24, lanes] = place
    listed = (jnp.broadcast_to(roots[...], (8, n_roots)) >= 0).astype(F32).astype(BF16)
    me = device[0]
    for at in range(0, n_all, 1024):
        shape = (n_roots, 1024)
        source = at // rank + iota(shape, 1) // rank
        if xor:
            source = jnp.bitwise_xor(source, me)
        usable = dot(listed, (iota(shape, 0) == source).astype(BF16))
        coef[:, at : at + 1024] = stack2(field[:vectors, at : at + 1024] * usable[0:1])[1]
        features(field[vectors:top, at : at + 1024], feats)
        to_rows(feats, src, at, 1024)
    features(pltpu.roll(tile0[...], LANES - 2 * rank, 1)[:coords], feats)
    tgt[:, :LANES] = feats[1, :, :LANES].astype(BF16)
    down = jnp.zeros((vectors, LANES), F32)
    for at in range(0, n_all, 512):
        kernel = jnp.exp2(dot(src[at : at + 512, :], tgt[:, :LANES]))
        down = down + apply_kernel(kernel, coef[:, at : at + 512], vectors)
    field[:vectors, :LANES] = down

    parent = field
    child = field2
    for level in range(1, LEVELS + 1):
        own = {1: c1, 2: c2, 3: c3}[level]
        width = own.shape[1]
        if level == 1:
            at = 2 * rim
            pieces = (
                (0, second_left, 0, group),
                (group, from_left, at, group),
                (2 * group, own, 0, group),
                (3 * group, from_right, at, group),
                (4 * group, second_right, 0, group),
            )
        else:
            at = 0 if level == 3 else rim
            pieces = (
                (0, from_left, at, rim),
                (rim, own, 0, width),
                (rim + width, from_right, at, rim),
            )
        for begin, ref, at, n in pieces:
            features(ref[vectors:top, at : at + n], feats)
            to_rows(feats, src, begin, n)
            if ref is own:
                tgt[:, :n] = feats[1, :, :n].astype(BF16)
            coef[:, begin : begin + n] = stack2(ref[:vectors, at : at + n])[1]
        base = (starts[level] - 1) * rank

        def far_group(q, carry, base=base, parent=parent, child=child):
            begin = q * group
            if not isinstance(q, int):
                begin = pl.multiple_of(begin, LANES)
            kernel = jnp.exp2(dot(src[pl.ds(begin, 5 * group), :], tgt[:, pl.ds(begin, group)]))
            mask = far_mask[:, pl.ds(base + begin, group)]
            kernel = jnp.concatenate(
                [kernel[rank * s : rank * (s + 1)] * mask[s : s + 1] for s in range(5 * FAN)],
                axis=0,
            )
            total = apply_kernel(kernel, coef[:, pl.ds(begin, 5 * group)], vectors)
            above = parent[:vectors, pl.ds((q // FAN) * group, group)]
            above = jnp.where(iota(above.shape, 1) // rank == q % FAN, above, 0.0)
            total = total + dot2(above, transfer[pl.ds(base + begin, group), :], NT)
            child[:vectors, pl.ds(begin, group)] = total
            return carry

        if width == group:
            far_group(0, 0)
        else:
            lax.fori_loop(0, width // group, far_group, 0, unroll=2)
        parent, child = child, parent

    span = FAN * leaf
    for g in range(n_points // span):
        big = block_rows(basis, g * span, leaf)
        out[:, g * span : (g + 1) * span] += dot2(parent[:vectors, g * group : (g + 1) * group], big)


def line(count, shift):
    return [(i, i + shift) for i in range(count) if 0 <= i + shift < count]


def body(points, rhs, leaf_basis, transfer, proxies, near_list, couple_list, root_list):
    count = lax.axis_size("leaf")
    device = lax.axis_index("leaf")
    rank = leaf_basis.shape[0]
    vectors, n_points = rhs.shape
    leaf = n_points // near_list.shape[0]
    group = FAN * rank
    starts = [(FAN**level - 1) // (FAN - 1) for level in range(LEVELS + 1)]
    n_transfer = transfer.shape[2]
    table = jnp.transpose(transfer, (2, 0, 1)).reshape(n_transfer * rank, rank)
    table = jnp.tile(table, (1, LANES // rank))
    flat_prox = proxies.reshape(proxies.shape[0] * rank, proxies.shape[2])

    vmem = pl.BlockSpec(memory_space=pltpu.VMEM)
    smem = pl.BlockSpec(memory_space=pltpu.SMEM)
    rim = 2 * group
    send = 2 * rim + group + REACH * leaf

    def shape(*dims):
        return jax.ShapeDtypeStruct(dims, F32)

    c3, c2, c1, tile0, right, left = pl.pallas_call(
        lambda *refs: upward_kernel(*refs, leaf=leaf, rank=rank, starts=starts),
        out_shape=(
            shape(ROWS, FAN**3 * rank),
            shape(ROWS, FAN**2 * rank),
            shape(ROWS, FAN * rank),
            shape(8, LANES),
            shape(ROWS, send),
            shape(ROWS, send),
        ),
        in_specs=[vmem] * 5,
        out_specs=(vmem,) * 6,
        name="upward",
    )(rhs, points, leaf_basis, table, flat_prox)

    xor = count & (count - 1) == 0
    if xor:
        gathered = tile0[None]
        step = 1
        while step < count:
            other = lax.ppermute(gathered, "leaf", [(i, i ^ step) for i in range(count)])
            gathered = jnp.concatenate([gathered, other], axis=0)
            step *= 2
    else:
        gathered = lax.all_gather(tile0, "leaf", axis=0)
    from_left = lax.ppermute(right, "leaf", line(count, 1))
    from_right = lax.ppermute(left, "leaf", line(count, -1))
    second_left = lax.ppermute(c1, "leaf", line(count, 2))
    second_right = lax.ppermute(c1, "leaf", line(count, -2))

    n_ext = n_points + 2 * REACH * leaf
    n_roots = root_list.shape[1]
    n_src = max(n_ext, n_roots * rank, 1024)
    n_couple = couple_list.shape[0]
    n_field = max(FAN**3 * rank, n_roots * rank)
    return pl.pallas_call(
        lambda *refs: final_kernel(*refs, leaf=leaf, rank=rank, starts=starts, xor=xor),
        out_shape=shape(vectors, n_points),
        in_specs=[smem] + [vmem] * 16,
        out_specs=vmem,
        scratch_shapes=[
            pltpu.VMEM((2, FEATS, n_src), F32),
            pltpu.VMEM((n_src, FEATS), BF16),
            pltpu.VMEM((FEATS, n_points), BF16),
            pltpu.VMEM((2 * vectors, n_src), BF16),
            pltpu.VMEM((8, n_points), F32),
            pltpu.VMEM((ROWS, n_couple * rank), F32),
            pltpu.VMEM((ROWS, n_field), F32),
            pltpu.VMEM((ROWS, n_field), F32),
        ],
        name="final",
    )(
        device.astype(jnp.int32)[None], rhs, points, leaf_basis, table, near_list, couple_list,
        root_list, c3, c2, c1, tile0, gathered, from_left, from_right, second_left, second_right,
    )


def solution(mesh):
    in_specs = (
        P(None, "leaf"),
        P(None, "leaf"),
        P(None, "leaf"),
        P(None, None, "leaf"),
        P(None, None, "leaf"),
        P("leaf", None),
        P("leaf", None),
        P("leaf", None),
    )
    out_specs = P(None, "leaf")
    return jax.shard_map(body, mesh=mesh, in_specs=in_specs, out_specs=out_specs, check_vma=False)
```

time: 222 us -> 63.8 us (0.29)
  the two profiles are of different devices: /device:TPU:0 before, /device:TPU:7 now
where the time goes in v1:
time: 63.8 us; the launch traced here: 63.4 us
  Pallas kernels  22.9 us (36%)
  starting transfers between devices  21.4 us (34%)
  waiting for transfers between devices  10.7 us (17%)
  local copies, waits for them, and re-layouts  6.3 us (10%)
  other arithmetic  1.99 us (3%)
    pallas_call x1, Pallas kernels, body(): pl.pallas_call(lambda *refs: final_kernel(*refs, leaf=leaf, rank=rank, st...  18.9 us
    ppermute x1, starting transfers between devices, body(): from_left = lax.ppermute(right, 'leaf', line(count, 1))  9.43 us
    ppermute x5, waiting for transfers between devices, body(): lax.ppermute(gathered, 'leaf', [(i, i ^ step) for i in range(count)])  6.44 us
    ppermute x5, starting transfers between devices, body(): lax.ppermute(gathered, 'leaf', [(i, i ^ step) for i in range(count)])  4.77 us
    ppermute x1, waiting for transfers between devices, body(): from_right = lax.ppermute(left, 'leaf', line(count, -1))  4.22 us
    pallas_call x1, Pallas kernels, body(): pl.pallas_call(lambda *refs: upward_kernel(*refs, leaf=leaf, rank=rank, s...  4.05 us
    ppermute x1, starting transfers between devices, body(): second_left = lax.ppermute(c1, 'leaf', line(count, 2))  3.1 us
    unnamed x20, local copies, waits for them, and re-layouts  2.73 us
  transfers between devices with their start and end apart: 9, of which 5 were waited for; matrix products, arithmetic and copies ran while one was open for 3% of the time, Pallas kernels for 0%

profile of v1, /device:TPU:7, one launch (start us, length us, event | category | flops | bytes accessed | tf_op | source)
XLA Modules:
  0.0 63.4 jit_solution(7568945442142458022)
XLA Ops:
  0.0 1.6 %copy.11 = f32[84,32,32]{1,0,2:T(8,128)S(1)} copy(f32[84,32,32]{0,2,1:T(8,128)} %bitcast.10) | data formatting | bytes 688128 | tf_op jit(solution)/shard_map/transpose | solution.py:348
  1.6 0.4 tile.10
  1.9 0.1 tile.11
  2.0 1.5 %copy.13.refs_3_.refs_4_ = f32[2688,128]{1,0:T(8,128)} copy(f32[2688,128]{0,1:T(8,128)S(1)} %bitcast.9) | data formatting | bytes 2752512 | tf_op jit(solution)/shard_map/tile | solution.py:349
  3.6 0.0 copy-start.5
  3.6 0.0 copy-start.6
  3.6 4.0 %upward.1 = (f32[24,2048]{1,0:T(8,128)}, f32[24,512]{1,0:T(8,128)}, f32[24,128]{1,0:T(8,128)}, f32[8,128]{1,0:T(8,128)}, f32[24,768]{1,0:T(8,128)}, /*index=5*/f32[24,768]{1,0:T(8,128)}) custom-call(f32[16,4096]{1,0:T(8,128)} %refs_1_.3, f32[3,4096]{1,0:T(4,128)} %refs_2_.3, f32[32,4096]{1,0:T(8,128)} %refs_3_.1, f32[2688,128]{1,0:T(8,128)} %copy.13.refs_3_.refs_4_, ...), custom_call_target="tpu_custom_call" | custom-call | tf_op jit(solution)/shard_map/upward/pallas_call | solution.py:360
  7.6 0.7 %collective-permute-start = (f32[1,8,128]{2,1,0:T(8,128)}, f32[1,8,128]{2,1,0:T(8,128)S(1)}, u32[]{:S(2)}, u32[]{:S(2)}) collective-permute-start(f32[1,8,128]{2,1,0:T(8,128)} %bitcast.11), channel_id=1, source_target_pairs={{0,1},{1,0},{2,3},{3,2},{4,5},{5,4},{6,7},{7,6},{8,9},{9,8},{10,11... | collective-permute-start | bytes 12296 | tf_op jit(solution)/shard_map/ppermute | solution.py:380
  8.3 0.7 %constant_dynamic-update-slice_fusion.4 = (f32[16,8,128]{2,1,0:T(8,128)S(1)}, f32[32,8,128]{2,1,0:T(8,128)S(1)}) fusion(f32[8,128]{1,0:T(8,128)} %get-tuple-element.14.refs_11_), kind=kLoop, calls=%fused_computation.5 | loop fusion | bytes 12288
  9.0 0.4 collective-permute-done
  9.3 0.7 %pad_maximum_fusion.2 = f32[2,8,128]{2,1,0:T(8,128)S(1)} fusion(f32[1,8,128]{2,1,0:T(8,128)S(1)} %collective-permute-done, f32[1,8,128]{2,1,0:T(8,128)} %bitcast.12), kind=kLoop, calls=%fused_computation.13 | loop fusion | flops 2048 | bytes 16384 | tf_op jit(solution)/shard_map/concatenate | solution.py:381
  10.0 0.3 collective-permute-start.1
  10.2 2.2 %collective-permute-done.1 = f32[2,8,128]{2,1,0:T(8,128)S(1)} collective-permute-done((f32[2,8,128]{2,1,0:T(8,128)S(1)}, f32[2,8,128]{2,1,0:T(8,128)S(1)}, u32[]{:S(2)}, u32[]{:S(2)}) %collective-permute-start.1) | collective-permute-done | bytes 8224 | tf_op jit(solution)/shard_map/ppermute | solution.py:380
  12.5 0.7 %pad_maximum_fusion.1 = f32[4,8,128]{2,1,0:T(8,128)S(1)} fusion(f32[2,8,128]{2,1,0:T(8,128)S(1)} %collective-permute-done.1, f32[1,8,128]{2,1,0:T(8,128)S(1)} %collective-permute-done, f32[1,8,128]{2,1,0:T(8,128)} %bitcast.13), kind=kLoop, calls=%fused_computation.12 | loop fusion | flops 8192 | bytes 32768 | tf_op jit(solution)/shard_map/concatenate | solution.py:381
  13.2 0.2 collective-permute-start.2
  13.4 2.4 %collective-permute-done.2 = f32[4,8,128]{2,1,0:T(8,128)S(1)} collective-permute-done((f32[4,8,128]{2,1,0:T(8,128)S(1)}, f32[4,8,128]{2,1,0:T(8,128)S(1)}, u32[]{:S(2)}, u32[]{:S(2)}) %collective-permute-start.2) | collective-permute-done | bytes 16416 | tf_op jit(solution)/shard_map/ppermute | solution.py:380
  15.7 0.7 %pad_maximum_fusion = f32[8,8,128]{2,1,0:T(8,128)S(1)} fusion(f32[4,8,128]{2,1,0:T(8,128)S(1)} %collective-permute-done.2, f32[2,8,128]{2,1,0:T(8,128)S(1)} %collective-permute-done.1, f32[1,8,128]{2,1,0:T(8,128)S(1)} %collective-permute-done, f32[1,8,128]{2,1,0:T(8,128)} %bitcast.14), kind=kLoop, calls=%fused_computation | loop fusion | flops 24576 | bytes 65536 | tf_op jit(solution)/shard_map/concatenate | solution.py:381
  16.4 1.3 %collective-permute-start.3 = (f32[8,8,128]{2,1,0:T(8,128)S(1)}, f32[8,8,128]{2,1,0:T(8,128)S(1)}, u32[]{:S(2)}, u32[]{:S(2)}) collective-permute-start(f32[8,8,128]{2,1,0:T(8,128)S(1)} %pad_maximum_fusion), channel_id=1, source_target_pairs={{0,8},{1,9},{2,10},{3,11},{4,12},{5,13},{6,14},{7,15},{8,0},{9,1},... | collective-permute-start | bytes 98312 | tf_op jit(solution)/shard_map/ppermute | solution.py:380
  17.7 1.5 %collective-permute-done.3 = f32[8,8,128]{2,1,0:T(8,128)S(1)} collective-permute-done((f32[8,8,128]{2,1,0:T(8,128)S(1)}, f32[8,8,128]{2,1,0:T(8,128)S(1)}, u32[]{:S(2)}, u32[]{:S(2)}) %collective-permute-start.3) | collective-permute-done | bytes 32800 | tf_op jit(solution)/shard_map/ppermute | solution.py:380
  19.2 2.3 %collective-permute-start.4 = (f32[16,8,128]{2,1,0:T(8,128)S(1)}, f32[16,8,128]{2,1,0:T(8,128)S(1)}, u32[]{:S(2)}, u32[]{:S(2)}) collective-permute-start(f32[16,8,128]{2,1,0:T(8,128)S(1)} %get-tuple-element.17), channel_id=1, source_target_pairs={{0,16},{1,17},{2,18},{3,19},{4,20},{5,21},{6,22},{7,23},{8,24},{9,... | collective-permute-start | bytes 196616 | tf_op jit(solution)/shard_map/ppermute | solution.py:380
  21.5 3.1 %collective-permute-start.7 = (f32[24,128]{1,0:T(8,128)}, f32[24,128]{1,0:T(8,128)S(1)}, u32[]{:S(2)}, u32[]{:S(2)}) collective-permute-start(f32[24,128]{1,0:T(8,128)} %get-tuple-element.13.refs_10_), channel_id=1, source_target_pairs={{0,2},{1,3},{2,4},{3,5},{4,6},{5,7},{6,8},{7,9},{8,10},{9,11},{10,... | collective-permute-start | bytes 36872 | tf_op jit(solution)/shard_map/ppermute | solution.py:387
  24.6 2.2 %collective-permute-start.8 = (f32[24,128]{1,0:T(8,128)}, f32[24,128]{1,0:T(8,128)S(1)}, u32[]{:S(2)}, u32[]{:S(2)}) collective-permute-start(f32[24,128]{1,0:T(8,128)} %get-tuple-element.13.refs_10_), channel_id=1, source_target_pairs={{2,0},{3,1},{4,2},{5,3},{6,4},{7,5},{8,6},{9,7},{10,8},{11,9},{12,... | collective-permute-start | bytes 36872 | tf_op jit(solution)/shard_map/ppermute | solution.py:388
  26.8 9.4 %collective-permute-start.5 = (f32[24,768]{1,0:T(8,128)}, f32[24,768]{1,0:T(8,128)S(1)}, u32[]{:S(2)}, u32[]{:S(2)}) collective-permute-start(f32[24,768]{1,0:T(8,128)} %get-tuple-element.15), channel_id=1, source_target_pairs={{0,1},{1,2},{2,3},{3,4},{4,5},{5,6},{6,7},{7,8},{8,9},{9,10},{10,1... | collective-permute-start | bytes 221192 | tf_op jit(solution)/shard_map/ppermute | solution.py:385
  36.2 1.9 %collective-permute-start.6 = (f32[24,768]{1,0:T(8,128)}, f32[24,768]{1,0:T(8,128)S(1)}, u32[]{:S(2)}, u32[]{:S(2)}) collective-permute-start(f32[24,768]{1,0:T(8,128)} %get-tuple-element.16), channel_id=1, source_target_pairs={{1,0},{2,1},{3,2},{4,3},{5,4},{6,5},{7,6},{8,7},{9,8},{10,9},{11,1... | collective-permute-start | bytes 221192 | tf_op jit(solution)/shard_map/ppermute | solution.py:386
  38.1 0.0 copy-done.5
  38.2 0.7 %copy.15.refs_6_ = s32[84,20]{1,0:T(8,128)} copy(s32[84,20]{0,1:T(8,128)S(1)} %copy-done.5) | data formatting | bytes 13440 | tf_op args[6]
  38.9 0.0 copy-done.6
  38.9 0.7 %copy.14.refs_5_ = s32[64,5]{1,0:T(8,128)} copy(s32[64,5]{0,1:T(8,128)S(1)} %copy-done.6) | data formatting | bytes 2560 | tf_op args[5]
  39.6 0.0 collective-permute-done.4
  39.6 0.0 copy-start
  39.6 0.0 collective-permute-done.7.refs_15_
  39.6 0.0 copy-start.3
  39.6 0.0 collective-permute-done.8.refs_16_
  39.6 0.0 copy-start.4
  39.7 0.0 collective-permute-done.5.refs_13_
  39.7 0.0 copy-start.1
  39.7 4.2 %collective-permute-done.6.refs_14_ = f32[24,768]{1,0:T(8,128)S(1)} collective-permute-done((f32[24,768]{1,0:T(8,128)}, f32[24,768]{1,0:T(8,128)S(1)}, u32[]{:S(2)}, u32[]{:S(2)}) %collective-permute-start.6) | collective-permute-done | bytes 73760 | tf_op jit(solution)/shard_map/ppermute | solution.py:386
  43.9 0.0 copy-start.2
  43.9 0.0 copy-done
  43.9 0.0 copy-done.3
  43.9 0.0 copy-done.4
  43.9 0.0 copy-done.1
  43.9 0.6 copy-done.2
  44.5 18.9 %final.1 = f32[16,4096]{1,0:T(8,128)} custom-call(s32[1]{0:T(128)} %bitcast.refs_0_, f32[16,4096]{1,0:T(8,128)} %refs_1_.3, f32[3,4096]{1,0:T(4,128)} %refs_2_.3, f32[32,4096]{1,0:T(8,128)} %refs_3_.1, f32[2688,128]{1,0:T(8,128)} %copy.13.refs_3_.refs_4_, s32[64,5]{1,0:T(8,128)} %copy.14.refs_5_, s32[84,20]{1,0:T(8,128)} %copy.15.refs_6_, s32[1,32]{1,0:T(1,128)} %refs_7_.1, ...), custom_call_target="tpu_custom_call" | custom-call | tf_op jit(solution)/shard_map/final/pallas_call | solution.py:395
  (5 shorter events, 0.0 us)
Async XLA Ops:
  3.6 34.6 %copy-start.5 = (s32[84,20]{0,1:T(8,128)S(1)}, s32[84,20]{0,1:T(8,128)}, u32[]{:S(2)}) copy-start(s32[84,20]{0,1:T(8,128)} %param.14) | copy-start | bytes 20164
  3.6 35.3 %copy-start.6 = (s32[64,5]{0,1:T(8,128)S(1)}, s32[64,5]{0,1:T(8,128)}, u32[]{:S(2)}) copy-start(s32[64,5]{0,1:T(8,128)} %param.13) | copy-start | bytes 3844
  7.6 1.7 %collective-permute-start = (f32[1,8,128]{2,1,0:T(8,128)}, f32[1,8,128]{2,1,0:T(8,128)S(1)}, u32[]{:S(2)}, u32[]{:S(2)}) collective-permute-start(f32[1,8,128]{2,1,0:T(8,128)} %bitcast.11), channel_id=1, source_target_pairs={{0,1},{1,0},{2,3},{3,2},{4,5},{5,4},{6,7},{7,6},{8,9},{9,8},{10,11... | collective-permute-start | bytes 12296 | tf_op jit(solution)/shard_map/ppermute | solution.py:380
  10.0 2.5 %collective-permute-start.1 = (f32[2,8,128]{2,1,0:T(8,128)S(1)}, f32[2,8,128]{2,1,0:T(8,128)S(1)}, u32[]{:S(2)}, u32[]{:S(2)}) collective-permute-start(f32[2,8,128]{2,1,0:T(8,128)S(1)} %pad_maximum_fusion.2), channel_id=1, source_target_pairs={{0,2},{1,3},{2,0},{3,1},{4,6},{5,7},{6,4},{7,5},{8,10},{9,11},{10,... | collective-permute-start | bytes 24584 | tf_op jit(solution)/shard_map/ppermute | solution.py:380
  13.2 2.6 %collective-permute-start.2 = (f32[4,8,128]{2,1,0:T(8,128)S(1)}, f32[4,8,128]{2,1,0:T(8,128)S(1)}, u32[]{:S(2)}, u32[]{:S(2)}) collective-permute-start(f32[4,8,128]{2,1,0:T(8,128)S(1)} %pad_maximum_fusion.1), channel_id=1, source_target_pairs={{0,4},{1,5},{2,6},{3,7},{4,0},{5,1},{6,2},{7,3},{8,12},{9,13},{10,... | collective-permute-start | bytes 49160 | tf_op jit(solution)/shard_map/ppermute | solution.py:380
  16.4 2.8 %collective-permute-start.3 = (f32[8,8,128]{2,1,0:T(8,128)S(1)}, f32[8,8,128]{2,1,0:T(8,128)S(1)}, u32[]{:S(2)}, u32[]{:S(2)}) collective-permute-start(f32[8,8,128]{2,1,0:T(8,128)S(1)} %pad_maximum_fusion), channel_id=1, source_target_pairs={{0,8},{1,9},{2,10},{3,11},{4,12},{5,13},{6,14},{7,15},{8,0},{9,1},... | collective-permute-start | bytes 98312 | tf_op jit(solution)/shard_map/ppermute | solution.py:380
  19.2 20.4 %collective-permute-start.4 = (f32[16,8,128]{2,1,0:T(8,128)S(1)}, f32[16,8,128]{2,1,0:T(8,128)S(1)}, u32[]{:S(2)}, u32[]{:S(2)}) collective-permute-start(f32[16,8,128]{2,1,0:T(8,128)S(1)} %get-tuple-element.17), channel_id=1, source_target_pairs={{0,16},{1,17},{2,18},{3,19},{4,20},{5,21},{6,22},{7,23},{8,24},{9,... | collective-permute-start | bytes 196616 | tf_op jit(solution)/shard_map/ppermute | solution.py:380
  21.5 18.1 %collective-permute-start.7 = (f32[24,128]{1,0:T(8,128)}, f32[24,128]{1,0:T(8,128)S(1)}, u32[]{:S(2)}, u32[]{:S(2)}) collective-permute-start(f32[24,128]{1,0:T(8,128)} %get-tuple-element.13.refs_10_), channel_id=1, source_target_pairs={{0,2},{1,3},{2,4},{3,5},{4,6},{5,7},{6,8},{7,9},{8,10},{9,11},{10,... | collective-permute-start | bytes 36872 | tf_op jit(solution)/shard_map/ppermute | solution.py:387
  24.6 15.0 %collective-permute-start.8 = (f32[24,128]{1,0:T(8,128)}, f32[24,128]{1,0:T(8,128)S(1)}, u32[]{:S(2)}, u32[]{:S(2)}) collective-permute-start(f32[24,128]{1,0:T(8,128)} %get-tuple-element.13.refs_10_), channel_id=1, source_target_pairs={{2,0},{3,1},{4,2},{5,3},{6,4},{7,5},{8,6},{9,7},{10,8},{11,9},{12,... | collective-permute-start | bytes 36872 | tf_op jit(solution)/shard_map/ppermute | solution.py:388
  26.8 12.9 %collective-permute-start.5 = (f32[24,768]{1,0:T(8,128)}, f32[24,768]{1,0:T(8,128)S(1)}, u32[]{:S(2)}, u32[]{:S(2)}) collective-permute-start(f32[24,768]{1,0:T(8,128)} %get-tuple-element.15), channel_id=1, source_target_pairs={{0,1},{1,2},{2,3},{3,4},{4,5},{5,6},{6,7},{7,8},{8,9},{9,10},{10,1... | collective-permute-start | bytes 221192 | tf_op jit(solution)/shard_map/ppermute | solution.py:385
  36.2 7.7 %collective-permute-start.6 = (f32[24,768]{1,0:T(8,128)}, f32[24,768]{1,0:T(8,128)S(1)}, u32[]{:S(2)}, u32[]{:S(2)}) collective-permute-start(f32[24,768]{1,0:T(8,128)} %get-tuple-element.16), channel_id=1, source_target_pairs={{1,0},{2,1},{3,2},{4,3},{5,4},{6,5},{7,6},{8,7},{9,8},{10,9},{11,1... | collective-permute-start | bytes 221192 | tf_op jit(solution)/shard_map/ppermute | solution.py:386
  39.6 4.3 %copy-start = (f32[32,8,128]{2,1,0:T(8,128)}, f32[32,8,128]{2,1,0:T(8,128)S(1)}, u32[]{:S(2)}) copy-start(f32[32,8,128]{2,1,0:T(8,128)S(1)} %constant_dynamic-update-slice_fusion.5.refs_12_) | copy-start | bytes 393220
  39.6 4.3 %copy-start.3 = (f32[24,128]{1,0:T(8,128)}, f32[24,128]{1,0:T(8,128)S(1)}, u32[]{:S(2)}) copy-start(f32[24,128]{1,0:T(8,128)S(1)} %collective-permute-done.7.refs_15_) | copy-start | bytes 36868
  39.6 4.3 %copy-start.4 = (f32[24,128]{1,0:T(8,128)}, f32[24,128]{1,0:T(8,128)S(1)}, u32[]{:S(2)}) copy-start(f32[24,128]{1,0:T(8,128)S(1)} %collective-permute-done.8.refs_16_) | copy-start | bytes 36868
  39.7 4.2 %copy-start.1 = (f32[24,768]{1,0:T(8,128)}, f32[24,768]{1,0:T(8,128)S(1)}, u32[]{:S(2)}) copy-start(f32[24,768]{1,0:T(8,128)S(1)} %collective-permute-done.5.refs_13_) | copy-start | bytes 221188
  43.9 0.6 copy-start.2

commit v2 on v0

v2 whole, which is shorter than its diff:
```python
import math

import jax
import jax.numpy as jnp
from jax import lax
from jax.experimental import pallas as pl
from jax.experimental.pallas import tpu as pltpu
from jax.sharding import PartitionSpec as P

LEVELS = 3
REACH = 2
FAN = 4
LANES = 128
ROWS = 24
FEATS = 32
SCALE = 10.0 * math.log2(math.e)
F32 = jnp.float32
BF16 = jnp.bfloat16

NN = (((1,), (0,)), ((), ()))
NT = (((1,), (1,)), ((), ()))


def dot(lhs, rhs, dims=NN):
    return lax.dot_general(lhs, rhs, dims, preferred_element_type=F32)


def iota(shape, axis):
    return lax.broadcasted_iota(jnp.int32, shape, axis)


def split2(value):
    high = value.astype(BF16)
    low = (value - high.astype(F32)).astype(BF16)
    return high, low


def split3(value):
    high = value.astype(BF16).astype(F32)
    rest = value - high
    mid = rest.astype(BF16).astype(F32)
    return high, mid, rest - mid


def stack2(value):
    high, low = split2(value)
    return jnp.concatenate([high, low], axis=0)


def dot2(both, high, low, dims=NN):
    rows = both.shape[0] // 2
    wide = dot(both, high, dims)
    return wide[:rows] + wide[rows:] + dot(both[:rows], low, dims)


def spread(clusters, width, begin, size):
    shape = (clusters, width)
    return (iota(shape, 0) == begin + iota(shape, 1) // size).astype(BF16)


def listed_mask(lists, begin, width, size):
    listed = (lists[...] >= 0).astype(F32).astype(BF16)
    return dot(listed, spread(lists.shape[1], width, begin, size))


def block_rows(basis, offset, leaf):
    part = basis[:, offset : offset + FAN * leaf]
    rank = part.shape[0]
    tiled = jnp.concatenate([part] * FAN, axis=0)
    keep = iota(tiled.shape, 0) // rank == iota(tiled.shape, 1) // leaf
    return split2(jnp.where(keep, tiled, 0.0))


def pick(groups):
    shape = (FEATS, FEATS)
    feature = iota(shape, 0)
    want = jnp.full(shape, -1, jnp.int32)
    for g, row in enumerate(groups):
        want = jnp.where(feature // 3 == g, row + feature % 3, want)
    return (iota(shape, 1) == want).astype(F32).astype(BF16)


def features(position):
    row = iota(position.shape, 0)
    centred = jnp.where(row < 3, position - 0.5, 0.0)
    norm = -SCALE * jnp.sum(centred * centred, axis=0, keepdims=True)
    tail = jnp.where((row >= 3) & (row < 6), 1.0, 0.0)
    for r, part in enumerate(split3(norm)):
        tail = jnp.where(row == r, part, tail)
    own = jnp.concatenate([*split3(centred), tail], axis=0).astype(BF16)
    other = jnp.concatenate([*split3(centred * (2.0 * SCALE)), tail], axis=0).astype(BF16)
    source = dot(pick((0, 0, 0, 8, 8, 16, 24, 27)), own)
    target = dot(pick((0, 8, 16, 0, 8, 0, 27, 24)), other)
    return source, target


def set_features(position, src, tgt, begin):
    n = position.shape[1]
    for at in range(0, n, 512):
        end = min(at + 512, n)
        source, target = features(position[:, at:end])
        if tgt is not None:
            tgt[:, begin + at : begin + end] = target.astype(BF16)
        if src is not None:
            for lane in range(0, end - at, LANES):
                to = begin + at + lane
                src[to : to + LANES, :] = jnp.transpose(source[:, lane : lane + LANES]).astype(
                    BF16
                )


def pad_rows(points):
    return jnp.concatenate([points, jnp.zeros((8 - points.shape[0], points.shape[1]), F32)], axis=0)


def fill_block(src, tgt, row, lane, n_rows, mask, size, high, low, at):
    kernel = jnp.exp2(dot(src[pl.ds(row, n_rows), :], tgt[:, pl.ds(lane, LANES)]))
    if mask is not None:
        kernel = jnp.concatenate(
            [kernel[size * s : size * (s + 1)] * mask[s : s + 1] for s in range(n_rows // size)],
            axis=0,
        )
    high[pl.ds(at, n_rows), :], low[pl.ds(at, n_rows), :] = split2(kernel)


def use_block(coef, row, n_rows, high, low, at):
    return dot2(coef[:, pl.ds(row, n_rows)], high[pl.ds(at, n_rows), :], low[pl.ds(at, n_rows), :])


def upward_kernel(
    device, rhs, points, basis, transfer, prox,
    c3, c2, c1, tile0, first, second, table_high, table_low,
    padded, moved, *, leaf, rank, starts,
):
    vectors = rhs.shape[0]
    coords = points.shape[0]
    span = FAN * leaf
    group = FAN * rank
    outs = {1: c1, 2: c2, 3: c3}

    n_clusters = transfer.shape[1]
    padded[...] = jnp.zeros(padded.shape, F32)
    padded[:, :n_clusters] = transfer[...]
    row = iota((8, LANES), 0)
    block = iota((8, LANES), 1) // rank
    for a in range(0, rank, FAN):
        flipped = jnp.transpose(padded[a * rank : (a + FAN) * rank, :])
        for t in range(0, n_clusters, 8):
            tile = flipped[t : t + 8]
            turns = [tile] + [pltpu.roll(tile, rank * s, 1) for s in range(1, FAN)]
            low = (t // FAN - 1) % FAN
            up = (t // FAN) % FAN
            in_low = (row < FAN) & (block == low)
            in_up = (row >= FAN) & (block == up)
            for j in range(FAN):
                value = jnp.where(in_up, turns[(up - j) % FAN], 0.0)
                value = jnp.where(in_low, turns[(low - j) % FAN], value)
                moved[t : t + 8, a + j, :] = value
    for t in range(0, n_clusters, FAN):
        rows = slice(t * rank, t * rank + group)
        table_high[rows, :], table_low[rows, :] = split2(
            moved[t : t + FAN].reshape(group, LANES)
        )

    for g in range(rhs.shape[1] // span):
        high, low = block_rows(basis, g * span, leaf)
        c3[:vectors, g * group : (g + 1) * group] = dot2(
            stack2(rhs[:, g * span : (g + 1) * span]), high, low, NT
        )
    for level in range(LEVELS, 0, -1):
        source = outs[level]
        count = FAN ** (level - 1)
        base = (starts[level] - 1) * rank
        per = min(FAN, count)
        width = per * group
        for h in range(count // per):
            begin = h * width
            rows = slice(base + begin, base + begin + width)
            merged = dot2(
                stack2(source[:vectors, begin : begin + width]),
                table_high[rows, :],
                table_low[rows, :],
            )
            if level > 1:
                outs[level - 1][:vectors, h * group : (h + 1) * group] = merged
            else:
                root = merged

    parts = jnp.concatenate(split3(prox[...]), axis=0).astype(BF16)
    clusters = prox.shape[1]
    n = coords * rank
    row = iota((8, LANES), 0)
    for level in range(LEVELS + 1):
        total = max(FAN**level * rank, LANES)
        step = min(total, 512)
        for begin in range(0, total, step):
            lines = dot(parts, spread(clusters, step, starts[level] + begin // rank, rank))
            lines = lines[:n] + lines[n : 2 * n] + lines[2 * n :]
            lines = jnp.where(iota(lines.shape, 0) % rank == iota(lines.shape, 1) % rank, lines, 0.0)
            rows = iota((8, step), 0)
            place = jnp.zeros((8, step), F32)
            for c in range(coords):
                line = jnp.sum(lines[c * rank : (c + 1) * rank], axis=0, keepdims=True)
                place = jnp.where(rows == c, line, place)
            if level == 0:
                root_place = place
            else:
                outs[level][vectors:, begin : begin + step] = place
    last = (FAN - 1) * rank
    tile = jnp.where(block == 0, pltpu.roll(root[:8], LANES - last, 1), 0.0)
    tile = jnp.where(block == 1, pltpu.roll(root[8:16], LANES - last + rank, 1), tile)
    tile = jnp.where(block == 2, pltpu.roll(root_place, 2 * rank, 1), tile)
    tile0[...] = tile

    rim = 2 * group
    halo = REACH * leaf

    def fill(send, tail):
        at = 0
        for ref, width in ((c3, rim), (c2, rim)):
            begin = ref.shape[1] - width if tail else 0
            send[:, at : at + width] = ref[:, begin : begin + width]
            at += width
        begin = points.shape[1] - halo if tail else 0
        send[:vectors, at : at + halo] = rhs[:, begin : begin + halo]
        send[vectors:, at : at + halo] = pad_rows(points[:, begin : begin + halo])

    @pl.when(device[0] % 2 == 0)
    def _():
        fill(first, True)
        fill(second, False)

    @pl.when(device[0] % 2 == 1)
    def _():
        fill(first, False)
        fill(second, True)

    at = 2 * rim + halo
    first[:, at : at + group] = c1[...]
    second[:, at : at + group] = c1[...]
    first[:8, at + group :] = tile
    first[8:, at + group :] = jnp.zeros((ROWS - 8, LANES), F32)


def middle_kernel(first, second, tile0, send, pair):
    width = second.shape[1]
    send[:, :width] = second[...]
    send[:, width:] = first[:, width - LANES : width]
    pair[0] = tile0[...]
    pair[1] = first[:8, width:]


def join_kernel(lower, upper, out):
    count = lower.shape[0]
    out[:count] = lower[...]
    out[count:] = upper[...]


def near_kernel(rhs, points, near, out, src, tgt, coef, mask, high, low, *, leaf, unroll):
    n_points = rhs.shape[1]
    halo = REACH * leaf
    count = n_points // halo
    set_features(pad_rows(points[...]), src, tgt, 0)
    coef[...] = stack2(rhs[...])
    for at in range(0, n_points, 1024):
        mask[:, at : at + 1024] = near_mask(near, at, 1024, leaf)

    def fill(g, carry):
        begin = pl.multiple_of(g * halo, LANES)
        fill_block(
            src, tgt, begin, pl.multiple_of(begin + halo, LANES), 3 * halo,
            mask[:, pl.ds(pl.multiple_of(begin + halo, LANES), halo)], leaf,
            high, low, pl.multiple_of(g * 3 * halo, LANES),
        )
        return carry

    def use(g, carry):
        begin = pl.multiple_of(g * halo, LANES)
        out[:, pl.ds(pl.multiple_of(begin + halo, LANES), halo)] = use_block(
            coef, begin, 3 * halo, high, low, pl.multiple_of(g * 3 * halo, LANES)
        )
        return carry

    lax.fori_loop(0, count - 2, fill, 0, unroll=unroll)
    lax.fori_loop(0, count - 2, use, 0, unroll=unroll)


def near_mask(near, begin, width, leaf):
    rows = listed_mask(near, begin // leaf, width, leaf)
    slots = rows.shape[0]
    odd = (iota((8, width), 1) // leaf) % 2 == 1
    even_rows = jnp.concatenate([rows, jnp.zeros((8 - slots, width), F32)], axis=0)
    return jnp.where(odd, pltpu.roll(even_rows, 1, 0), even_rows)


def far_kernel(
    c3, couple, basis, out, big_high, big_low, src, tgt, coef, mask, high, low,
    *, leaf, rank, base, unroll,
):
    group = FAN * rank
    vectors = out.shape[0]
    width = c3.shape[1]
    set_features(c3[vectors:, :], src, tgt, 0)
    coef[...] = stack2(c3[:vectors, :])
    slots = couple.shape[0]
    for at in range(0, width, 512):
        mask[:slots, at : at + 512] = listed_mask(couple, base + at // rank, 512, rank)

    def fill(q, carry):
        begin = pl.multiple_of(q * group, LANES)
        target = pl.multiple_of(begin + 2 * group, LANES)
        fill_block(
            src, tgt, begin, target, 5 * group, mask[:, pl.ds(target, group)], rank,
            high, low, pl.multiple_of(q * 5 * group, LANES),
        )
        return carry

    def use(q, carry):
        begin = pl.multiple_of(q * group, LANES)
        out[:, pl.ds(pl.multiple_of(begin + 2 * group, LANES), group)] = use_block(
            coef, begin, 5 * group, high, low, pl.multiple_of(q * 5 * group, LANES)
        )
        return carry

    count = width // group - 4
    lax.fori_loop(0, count, fill, 0, unroll=unroll)
    lax.fori_loop(0, count, use, 0, unroll=unroll)
    span = FAN * leaf
    for g in range(basis.shape[1] // span):
        rows = slice(g * group, (g + 1) * group)
        big_high[rows, :], big_low[rows, :] = block_rows(basis, g * span, leaf)


def edge_kernel(
    device, first, second, c3, c2, rhs, points, near, couple,
    near_edge, g3_edge, g2, ext, src, tgt, coef, high, low,
    *, leaf, rank, starts,
):
    group = FAN * rank
    rim = 2 * group
    halo = REACH * leaf
    vectors = rhs.shape[0]
    n3 = c3.shape[1]
    n2 = c2.shape[1]
    n_points = rhs.shape[1]
    l3 = 0
    r3 = l3 + 3 * rim
    l2 = r3 + 3 * rim
    ln = l2 + n2 + 2 * rim
    rn = ln + 3 * halo

    def rims(left, right):
        ext[:, l3 : l3 + rim] = left[:, :rim]
        ext[:, r3 + 2 * rim : r3 + 3 * rim] = right[:, :rim]
        ext[:, l2 : l2 + rim] = left[:, rim : 2 * rim]
        ext[:, l2 + rim + n2 : l2 + 2 * rim + n2] = right[:, rim : 2 * rim]
        ext[:, ln : ln + halo] = left[:, 2 * rim : 2 * rim + halo]
        ext[:, rn + 2 * halo : rn + 3 * halo] = right[:, 2 * rim : 2 * rim + halo]

    @pl.when(device[0] % 2 == 0)
    def _():
        rims(second, first)

    @pl.when(device[0] % 2 == 1)
    def _():
        rims(first, second)

    ext[:, l3 + rim : l3 + 3 * rim] = c3[:, : 2 * rim]
    ext[:, r3 : r3 + 2 * rim] = c3[:, n3 - 2 * rim :]
    ext[:, l2 + rim : l2 + rim + n2] = c2[...]
    for to, begin in ((ln + halo, 0), (rn, n_points - 2 * halo)):
        ext[:vectors, to : to + 2 * halo] = rhs[:, begin : begin + 2 * halo]
        ext[vectors:, to : to + 2 * halo] = pad_rows(points[:, begin : begin + 2 * halo])
    set_features(ext[vectors:, :], src, tgt, 0)
    coef[...] = stack2(ext[:vectors, :])
    base3 = starts[3] - 1
    base2 = starts[2] - 1
    n_leaves = n_points // leaf
    jobs = []
    for i in range(2):
        for to, begin, cluster in ((i, l3, i * FAN), (2 + i, r3, (n3 // group - 2 + i) * FAN)):
            jobs.append((g3_edge, to * group, begin + i * group, 5 * group, rim, base3 + cluster))
    for q in range(n2 // group):
        jobs.append((g2, q * group, l2 + q * group, 5 * group, rim, base2 + q * FAN))
    jobs.append((near_edge, 0, ln, 3 * halo, halo, 0))
    jobs.append((near_edge, halo, rn, 3 * halo, halo, n_leaves - 2))
    at = 0
    for out, to, begin, n_rows, ahead, cluster in jobs:
        if out is near_edge:
            mask, size = near_mask(near, cluster * leaf, halo, leaf), leaf
        else:
            mask, size = listed_mask(couple, cluster, group, rank), rank
        fill_block(src, tgt, begin, begin + ahead, n_rows, mask, size, high, low, at)
        at += n_rows
    at = 0
    for out, to, begin, n_rows, ahead, cluster in jobs:
        out[:, to : to + LANES] = use_block(coef, begin, n_rows, high, low, at)
        at += n_rows


def final_kernel(
    device, gathered, roots, tile0, c1, first, second, third, couple, near, near_edge,
    g3, g3_edge, g2, table_high, table_low, big_high, big_low, out,
    ext, src, tgt, coef, high, low, *, leaf, rank, starts, xor,
):
    group = FAN * rank
    vectors = out.shape[0]
    me = device[0]
    n_roots = roots.shape[1]
    n_all = n_roots * rank
    here = 2 * (2 * group) + REACH * leaf
    block = iota((8, LANES), 1) // rank
    for at in range(0, n_roots, FAN):
        tiles = [jnp.zeros((8, LANES), F32)] * 3
        for j in range(FAN):
            value = gathered[at + j]
            for i in range(3):
                turn = ((j - i) % FAN) * rank
                turned = pltpu.roll(value, turn, 1) if turn else value
                tiles[i] = jnp.where(block == j, turned, tiles[i])
        lanes = slice(at * rank, at * rank + LANES)
        for i in range(3):
            ext[8 * i : 8 * i + 8, lanes] = tiles[i]
    one = n_all

    def order(parts):
        for i, part in enumerate(parts):
            ext[:, one + i * group : one + (i + 1) * group] = part

    own = first[:, here : here + group]
    near_by = second[:, here : here + group]
    beyond = second[:, here + group : here + 2 * group]

    @pl.when(me % 2 == 0)
    def _():
        order((beyond, near_by, c1[...], own, third[...]))

    @pl.when(me % 2 == 1)
    def _():
        order((third[...], own, c1[...], near_by, beyond))

    root = one + 5 * group
    ext[vectors:, root : root + LANES] = pltpu.roll(tile0[...], rank, 1)
    ext[:vectors, root : root + LANES] = jnp.zeros((vectors, LANES), F32)
    set_features(ext[vectors:, :root], src, None, 0)
    set_features(ext[vectors:, one + 2 * group : one + 3 * group], None, tgt, 0)
    set_features(ext[vectors:, root : root + LANES], None, tgt, LANES)
    listed = (jnp.broadcast_to(roots[...], (8, n_roots)) >= 0).astype(F32).astype(BF16)
    for at in range(0, n_all, 512):
        shape = (n_roots, 512)
        source = at // rank + iota(shape, 1) // rank
        if xor:
            source = jnp.bitwise_xor(source, me)
        usable = dot(listed, (iota(shape, 0) == source).astype(F32).astype(BF16))
        coef[:, at : at + 512] = stack2(ext[:vectors, at : at + 512] * usable[0:1])
    coef[:, one:root] = stack2(ext[:vectors, one:root])
    for at in range(0, n_all, 512):
        fill_block(src, tgt, at, LANES, 512, None, rank, high, low, at)
    fill_block(
        src, tgt, one, 0, 5 * group, listed_mask(couple, 0, group, rank), rank, high, low, one
    )
    f0 = jnp.zeros((vectors, LANES), F32)
    for at in range(0, n_all, 512):
        f0 = f0 + use_block(coef, at, 512, high, low, at)
    g1 = use_block(coef, one, 5 * group, high, low, one)

    def down(above, level, q):
        begin = (starts[level] - 1) * rank + q * group
        rows = slice(begin, begin + group)
        return dot2(above, table_high[rows, :], table_low[rows, :], NT)

    f1 = stack2(g1 + down(stack2(f0), 1, 0))
    f2 = []
    for q in range(FAN):
        f2.append(stack2(g2[:, q * group : (q + 1) * group] + down(f1, 2, q)))
    count = FAN * FAN
    span = FAN * leaf
    halo = REACH * leaf
    for q in range(count):
        if q < 2:
            total = g3_edge[:, q * group : (q + 1) * group]
        elif q >= count - 2:
            to = (q - count + 4) * group
            total = g3_edge[:, to : to + group]
        else:
            total = g3[:, q * group : (q + 1) * group]
        f3 = stack2(total + down(f2[q // FAN], 3, q))
        rows = slice(q * group, (q + 1) * group)
        value = dot2(f3, big_high[rows, :], big_low[rows, :])
        if q == 0:
            base = jnp.concatenate([near_edge[:, :halo], near[:, halo:span]], axis=1)
        elif q == count - 1:
            base = jnp.concatenate(
                [near[:, q * span : (q + 1) * span - halo], near_edge[:, halo:]], axis=1
            )
        else:
            base = near[:, q * span : (q + 1) * span]
        out[:, q * span : (q + 1) * span] = base + value


def largest_unroll(count, most):
    return max(d for d in range(1, most + 1) if count % d == 0)


def body(points, rhs, leaf_basis, transfer, proxies, near_list, couple_list, root_list):
    count = lax.axis_size("leaf")
    device = lax.axis_index("leaf").astype(jnp.int32)[None]
    rank = leaf_basis.shape[0]
    vectors, n_points = rhs.shape
    n_leaves = near_list.shape[0]
    leaf = n_points // n_leaves
    group = FAN * rank
    rim = 2 * group
    halo = REACH * leaf
    starts = [(FAN**level - 1) // (FAN - 1) for level in range(LEVELS + 1)]
    n_clusters = transfer.shape[2]
    n3 = FAN**3 * rank
    n2 = FAN**2 * rank
    flat_transfer = transfer.reshape(rank * rank, n_clusters)
    flat_prox = proxies.reshape(proxies.shape[0] * rank, proxies.shape[2])
    near_t = near_list.T
    couple_t = couple_list.T

    vmem = pl.BlockSpec(memory_space=pltpu.VMEM)
    smem = pl.BlockSpec(memory_space=pltpu.SMEM)

    def shape(*dims, dtype=F32):
        return jax.ShapeDtypeStruct(dims, dtype)

    def call(kernel, n_in, outs, scratch, name, mib, scalar=True):
        return pl.pallas_call(
            kernel,
            out_shape=outs,
            in_specs=([smem] if scalar else []) + [vmem] * n_in,
            out_specs=jax.tree.map(lambda _: vmem, outs),
            scratch_shapes=scratch,
            compiler_params=pltpu.CompilerParams(vmem_limit_bytes=mib << 20),
            name=name,
        )

    padded_clusters = -(-n_clusters // 8) * 8
    width = 2 * rim + halo + group
    c3, c2, c1, tile0, to_first, to_second, table_high, table_low = call(
        lambda *refs: upward_kernel(*refs, leaf=leaf, rank=rank, starts=starts),
        5,
        (
            shape(ROWS, n3),
            shape(ROWS, n2),
            shape(ROWS, group),
            shape(8, LANES),
            shape(ROWS, width + LANES),
            shape(ROWS, width),
            shape(n_clusters * rank, LANES, dtype=BF16),
            shape(n_clusters * rank, LANES, dtype=BF16),
        ),
        [pltpu.VMEM((rank * rank, LANES), F32), pltpu.VMEM((padded_clusters, rank, LANES), F32)],
        "upward",
        16,
    )(device, rhs, points, leaf_basis, flat_transfer, flat_prox)

    def swap(value, step):
        return lax.ppermute(value, "leaf", [(i, i ^ step) for i in range(count)])

    first = swap(to_first, 1)
    send, gathered = call(
        middle_kernel,
        3,
        (shape(ROWS, width + group), shape(2, 8, LANES)),
        [],
        "middle",
        2,
        scalar=False,
    )(first, to_second, tile0)
    xor = count & (count - 1) == 0

    def join(lower, upper):
        return call(
            join_kernel, 2, shape(2 * lower.shape[0], 8, LANES), [], "join", 2, scalar=False
        )(lower, upper)

    if xor:
        step = 2
        while step < count:
            other = swap(gathered, step)
            if step == 2:
                pairs = [(i, i + 1) for i in range(1, count - 1, 2)]
                second = lax.ppermute(send, "leaf", pairs + [(j, i) for i, j in pairs])
                third = swap(second[:, width - group : width], 1)
            gathered = join(gathered, other)
            step *= 2
    else:
        gathered = lax.all_gather(tile0, "leaf", axis=0)
        pairs = [(i, i + 1) for i in range(1, count - 1, 2)]
        second = lax.ppermute(send, "leaf", pairs + [(j, i) for i, j in pairs])
        third = swap(second[:, width - group : width], 1)

    n_near = n_points // halo - 2
    near = call(
        lambda *refs: near_kernel(*refs, leaf=leaf, unroll=largest_unroll(n_near, 16)),
        3,
        shape(vectors, n_points),
        [
            pltpu.VMEM((n_points, FEATS), BF16),
            pltpu.VMEM((FEATS, n_points), BF16),
            pltpu.VMEM((2 * vectors, n_points), BF16),
            pltpu.VMEM((8, n_points), F32),
            pltpu.VMEM((n_near * 3 * halo, LANES), BF16),
            pltpu.VMEM((n_near * 3 * halo, LANES), BF16),
        ],
        "near",
        16,
        scalar=False,
    )(rhs, points, near_t)

    n_far = FAN**2 - 4
    span = FAN * leaf
    g3, big_high, big_low = call(
        lambda *refs: far_kernel(
            *refs, leaf=leaf, rank=rank, base=starts[3] - 1, unroll=largest_unroll(n_far, 12)
        ),
        3,
        (
            shape(vectors, n3),
            shape(n_points // span * group, span, dtype=BF16),
            shape(n_points // span * group, span, dtype=BF16),
        ),
        [
            pltpu.VMEM((n3, FEATS), BF16),
            pltpu.VMEM((FEATS, n3), BF16),
            pltpu.VMEM((2 * vectors, n3), BF16),
            pltpu.VMEM((ROWS, n3), F32),
            pltpu.VMEM((n_far * 5 * group, LANES), BF16),
            pltpu.VMEM((n_far * 5 * group, LANES), BF16),
        ],
        "far",
        16,
        scalar=False,
    )(c3, couple_t, leaf_basis)

    n_ext = 6 * rim + n2 + 2 * rim + 6 * halo
    n_rows = (4 + n2 // group) * 5 * group + 2 * 3 * halo
    near_edge, g3_edge, g2 = call(
        lambda *refs: edge_kernel(*refs, leaf=leaf, rank=rank, starts=starts),
        8,
        (shape(vectors, 2 * halo), shape(vectors, 2 * rim), shape(vectors, n2)),
        [
            pltpu.VMEM((ROWS, n_ext), F32),
            pltpu.VMEM((n_ext, FEATS), BF16),
            pltpu.VMEM((FEATS, n_ext), BF16),
            pltpu.VMEM((2 * vectors, n_ext), BF16),
            pltpu.VMEM((n_rows, LANES), BF16),
            pltpu.VMEM((n_rows, LANES), BF16),
        ],
        "edge",
        16,
    )(device, first, second, c3, c2, rhs, points, near_t, couple_t)

    n_all = count * rank
    n_top = n_all + 5 * group
    return call(
        lambda *refs: final_kernel(*refs, leaf=leaf, rank=rank, starts=starts, xor=xor),
        17,
        shape(vectors, n_points),
        [
            pltpu.VMEM((ROWS, n_top + LANES), F32),
            pltpu.VMEM((n_top, FEATS), BF16),
            pltpu.VMEM((FEATS, 2 * LANES), BF16),
            pltpu.VMEM((2 * vectors, n_top), BF16),
            pltpu.VMEM((n_top, LANES), BF16),
            pltpu.VMEM((n_top, LANES), BF16),
        ],
        "final",
        16,
    )(
        device, gathered, root_list, tile0, c1, first, second, third, couple_t, near, near_edge,
        g3, g3_edge, g2, table_high, table_low, big_high, big_low,
    )


def solution(mesh):
    in_specs = (
        P(None, "leaf"),
        P(None, "leaf"),
        P(None, "leaf"),
        P(None, None, "leaf"),
        P(None, None, "leaf"),
        P("leaf", None),
        P("leaf", None),
        P("leaf", None),
    )
    out_specs = P(None, "leaf")
    return jax.shard_map(body, mesh=mesh, in_specs=in_specs, out_specs=out_specs, check_vma=False)
```

time: 222 us -> 38.6 us (0.17)
  the two profiles are of different devices: /device:TPU:0 before, /device:TPU:17 now
where the time goes in v2:
time: 38.6 us; the launch traced here: 38.3 us
  Pallas kernels  14.1 us (37%)
  starting transfers between devices  13.1 us (34%)
  waiting for transfers between devices  5.6 us (15%)
  local copies, waits for them, and re-layouts  5.34 us (14%)
    ppermute x6, starting transfers between devices, swap(): return lax.ppermute(value, 'leaf', [(i, i ^ step) for i in range(count)])  7.16 us
    ppermute x1, starting transfers between devices, body(): second = lax.ppermute(send, 'leaf', pairs + [(j, i) for i, j in pairs])  5.97 us
    unnamed x22, local copies, waits for them, and re-layouts  5.34 us
    pallas_call x1, Pallas kernels, body(): call(lambda *refs: final_kernel(*refs, leaf=leaf, rank=rank, starts=start...  4.65 us
    ppermute x6, waiting for transfers between devices, swap(): return lax.ppermute(value, 'leaf', [(i, i ^ step) for i in range(count)])  3.58 us
    pallas_call x1, Pallas kernels, body(): call(lambda *refs: near_kernel(*refs, leaf=leaf, unroll=largest_unroll(n_...  3.48 us
    pallas_call x1, Pallas kernels, body(): call(lambda *refs: upward_kernel(*refs, leaf=leaf, rank=rank, starts=star...  2.44 us
    ppermute x1, waiting for transfers between devices, body(): second = lax.ppermute(send, 'leaf', pairs + [(j, i) for i, j in pairs])  2.02 us
  transfers between devices with their start and end apart: 7, of which 4 were waited for; matrix products, arithmetic and copies ran while one was open for 0% of the time, Pallas kernels for 18%

profile of v2, /device:TPU:17, one launch (start us, length us, event | category | flops | bytes accessed | tf_op | source)
XLA Modules:
  0.0 38.3 jit_solution(15848313183584921426)
XLA Ops:
  0.0 0.0 copy-start
  0.0 0.9 %copy-done = f32[16,4096]{1,0:T(8,128)S(1)} copy-done((f32[16,4096]{1,0:T(8,128)S(1)}, f32[16,4096]{1,0:T(8,128)}, u32[]{:S(2)}) %copy-start) | copy-done | bytes 262168
  1.0 0.0 copy-start.2
  1.0 1.0 %copy-done.2 = f32[32,4096]{1,0:T(8,128)S(1)} copy-done((f32[32,4096]{1,0:T(8,128)S(1)}, f32[32,4096]{1,0:T(8,128)}, u32[]{:S(2)}) %copy-start.2) | copy-done | bytes 524312
  2.0 0.0 copy-start.4
  2.0 0.8 %copy-done.4 = f32[3,4096]{1,0:T(4,128)S(1)} copy-done((f32[3,4096]{1,0:T(4,128)S(1)}, f32[3,4096]{1,0:T(4,128)}, u32[]{:S(2)}) %copy-start.4) | copy-done | bytes 49176
  2.8 0.0 copy-start.6
  2.8 1.0 %copy-done.6 = f32[32,32,84]{2,1,0:T(8,128)S(1)} copy-done((f32[32,32,84]{2,1,0:T(8,128)S(1)}, f32[32,32,84]{2,1,0:T(8,128)}, u32[]{:S(2)}) %copy-start.6) | copy-done | bytes 344088
  3.9 0.0 copy-start.8
  3.9 0.8 %copy-done.8 = f32[3,32,85]{2,1,0:T(8,128)S(1)} copy-done((f32[3,32,85]{2,1,0:T(8,128)S(1)}, f32[3,32,85]{2,1,0:T(8,128)}, u32[]{:S(2)}) %copy-start.8) | copy-done | bytes 32664
  4.7 0.0 copy-start.5
  4.7 0.0 copy-start.9
  4.7 2.4 %upward.1 = (f32[24,2048]{1,0:T(8,128)S(1)}, f32[24,512]{1,0:T(8,128)S(1)}, f32[24,128]{1,0:T(8,128)S(1)}, f32[8,128]{1,0:T(8,128)S(1)}, f32[24,896]{1,0:T(8,128...) custom-call(s32[1]{0:T(128)} %bitcast.refs_0_, ...), custom_call_target="tpu_custom_call" | custom-call | tf_op jit(solution)/shard_map/upward/pallas_call | solution.py:543
  7.1 0.0 copy-start.1
  7.1 0.0 copy-start.3
  7.1 0.7 %collective-permute-start = (f32[24,896]{1,0:T(8,128)S(1)}, f32[24,896]{1,0:T(8,128)S(1)}, u32[]{:S(2)}, u32[]{:S(2)}) collective-permute-start(f32[24,896]{1,0:T(8,128)S(1)} %get-tuple-element.21), channel_id=1, source_target_pairs={{0,1},{1,0},{2,3},{3,2},{4,5},{5,4},{6,7},{7,6},{8,9},{9,8},{10,11... | collective-permute-start | bytes 258056 | tf_op jit(solution)/shard_map/ppermute | solution.py:562
  7.9 0.9 %collective-permute-done.first.refs_1_.refs_5_ = f32[24,896]{1,0:T(8,128)S(1)} collective-permute-done((f32[24,896]{1,0:T(8,128)S(1)}, f32[24,896]{1,0:T(8,128)S(1)}, u32[]{:S(2)}, u32[]{:S(2)}) %collective-permute-start) | collective-permute-done | bytes 86048 | tf_op jit(solution)/shard_map/ppermute | solution.py:562
  8.8 1.2 %collective-permute-start.1 = (f32[2,8,128]{2,1,0:T(8,128)S(1)}, f32[2,8,128]{2,1,0:T(8,128)S(1)}, u32[]{:S(2)}, u32[]{:S(2)}) collective-permute-start(f32[2,8,128]{2,1,0:T(8,128)S(1)} %get-tuple-element.24.lower), channel_id=1, source_target_pairs={{0,2},{1,3},{2,0},{3,1},{4,6},{5,7},{6,4},{7,5},{8,10},{9,11},{10,... | collective-permute-start | bytes 24584 | tf_op jit(solution)/shard_map/ppermute | solution.py:562
  10.1 1.3 %collective-permute-done.1.upper = f32[2,8,128]{2,1,0:T(8,128)S(1)} collective-permute-done((f32[2,8,128]{2,1,0:T(8,128)S(1)}, f32[2,8,128]{2,1,0:T(8,128)S(1)}, u32[]{:S(2)}, u32[]{:S(2)}) %collective-permute-start.1) | collective-permute-done | bytes 8224 | tf_op jit(solution)/shard_map/ppermute | solution.py:562
  11.3 1.2 %collective-permute-start.2 = (f32[4,8,128]{2,1,0:T(8,128)S(1)}, f32[4,8,128]{2,1,0:T(8,128)S(1)}, u32[]{:S(2)}, u32[]{:S(2)}) collective-permute-start(f32[4,8,128]{2,1,0:T(8,128)S(1)} %join.4.lower), channel_id=1, source_target_pairs={{0,4},{1,5},{2,6},{3,7},{4,0},{5,1},{6,2},{7,3},{8,12},{9,13},{10,... | collective-permute-start | bytes 49160 | tf_op jit(solution)/shard_map/ppermute | solution.py:562
  12.6 1.4 %collective-permute-done.2.upper = f32[4,8,128]{2,1,0:T(8,128)S(1)} collective-permute-done((f32[4,8,128]{2,1,0:T(8,128)S(1)}, f32[4,8,128]{2,1,0:T(8,128)S(1)}, u32[]{:S(2)}, u32[]{:S(2)}) %collective-permute-start.2) | collective-permute-done | bytes 16416 | tf_op jit(solution)/shard_map/ppermute | solution.py:562
  13.9 1.3 %collective-permute-start.3 = (f32[8,8,128]{2,1,0:T(8,128)S(1)}, f32[8,8,128]{2,1,0:T(8,128)S(1)}, u32[]{:S(2)}, u32[]{:S(2)}) collective-permute-start(f32[8,8,128]{2,1,0:T(8,128)S(1)} %join.5.lower), channel_id=1, source_target_pairs={{0,8},{1,9},{2,10},{3,11},{4,12},{5,13},{6,14},{7,15},{8,0},{9,1},... | collective-permute-start | bytes 98312 | tf_op jit(solution)/shard_map/ppermute | solution.py:562
  15.2 6.0 %collective-permute-start.5 = (f32[24,896]{1,0:T(8,128)S(1)}, f32[24,896]{1,0:T(8,128)S(1)}, u32[]{:S(2)}, u32[]{:S(2)}) collective-permute-start(f32[24,896]{1,0:T(8,128)S(1)} %get-tuple-element.26), channel_id=1, source_target_pairs={{1,2},{3,4},{5,6},{7,8},{9,10},{11,12},{13,14},{15,16},{17,18},{19... | collective-permute-start | bytes 258056 | tf_op jit(solution)/shard_map/ppermute | solution.py:587
  21.2 0.0 collective-permute-done.3.upper
  21.2 0.1 collective-permute-start.4
  21.4 2.0 %collective-permute-done.5.refs_2_.refs_6_ = f32[24,896]{1,0:T(8,128)S(1)} collective-permute-done((f32[24,896]{1,0:T(8,128)S(1)}, f32[24,896]{1,0:T(8,128)S(1)}, u32[]{:S(2)}, u32[]{:S(2)}) %collective-permute-start.5) | collective-permute-done | bytes 86048 | tf_op jit(solution)/shard_map/ppermute | solution.py:587
  23.4 2.5 %collective-permute-start.6 = (f32[24,128]{1,0:T(8,128)S(1)}, f32[24,128]{1,0:T(8,128)S(1)}, u32[]{:S(2)}, u32[]{:S(2)}) collective-permute-start(f32[24,128]{1,0:T(8,128)S(1)} %slice.4), channel_id=1, source_target_pairs={{0,1},{1,0},{2,3},{3,2},{4,5},{5,4},{6,7},{7,6},{8,9},{9,8},{10,11... | collective-permute-start | bytes 36872 | tf_op jit(solution)/shard_map/ppermute | solution.py:562
  25.9 0.0 copy-done.5
  25.9 0.0 copy-done.9
  25.9 0.0 copy-done.1
  25.9 0.0 copy-start.7
  25.9 3.5 %near.1.refs_9_ = f32[16,4096]{1,0:T(8,128)S(1)} custom-call(f32[16,4096]{1,0:T(8,128)S(1)} %copy-done.1, f32[3,4096]{1,0:T(4,128)S(1)} %copy-done.5, s32[5,64]{1,0:T(8,128)S(1)} %bitcast.10), custom_call_target="tpu_custom_call" | custom-call | tf_op jit(solution)/shard_map/near/pallas_call | solution.py:598
  29.4 0.0 copy-done.3
  29.4 0.0 copy-done.7
  29.4 2.0 %far.1 = (f32[16,2048]{1,0:T(8,128)S(1)}, bf16[2048,256]{1,0:T(8,128)(2,1)S(1)}, bf16[2048,256]{1,0:T(8,128)(2,1)S(1)}) custom-call(f32[24,2048]{1,0:T(8,128)S(1)} %get-tuple-element.27.refs_3_.refs_0_, s32[20,84]{1,0:T(8,128)S(1)} %bitcast.6, f32[32,4096]{1,0:T(8,128)S(1)} %copy-done.3), custom_call_target="tpu_custom_call" | custom-call | tf_op jit(solution)/shard_map/far/pallas_call | solution.py:617
  31.4 1.5 %edge.1 = (f32[16,256]{1,0:T(8,128)S(1)}, f32[16,512]{1,0:T(8,128)S(1)}, f32[16,512]{1,0:T(8,128)S(1)}) custom-call(s32[1]{0:T(128)} %bitcast.refs_0_, f32[24,896]{1,0:T(8,128)S(1)} %collective-permute-done.first.refs_1_.refs_5_, f32[24,896]{1,0:T(8,128)S(1)} %collective-permute-done.5.refs_2_.refs_6_, f32[24,2048]{1,0:T(8,128)S(1)} %get-tuple-element.27.refs_3_.refs_0_, ...), custom_call_target="tpu_custom_call" | custom-call | tf_op jit(solution)/shard_map/edge/pallas_call | solution.py:642
  32.9 0.0 collective-permute-done.4.upper
  33.0 0.0 collective-permute-done.6.refs_7_
  33.0 0.0 copy-start.10
  33.0 0.6 %copy-done.10 = s32[1,32]{1,0:T(1,128)S(1)} copy-done((s32[1,32]{1,0:T(1,128)S(1)}, s32[1,32]{1,0:T(1,128)}, u32[]{:S(2)}) %copy-start.10) | copy-done | bytes 152
  33.6 4.6 %final.1 = f32[16,4096]{1,0:T(8,128)} custom-call(s32[1]{0:T(128)} %bitcast.refs_0_, f32[32,8,128]{2,1,0:T(8,128)S(1)} %join.7.refs_1_, s32[1,32]{1,0:T(1,128)S(1)} %copy-done.10, f32[8,128]{1,0:T(8,128)S(1)} %get-tuple-element.23.tile0.refs_3_, f32[24,128]{1,0:T(8,128)S(1)} %get-tuple-element.25.refs_4_, ...), custom_call_target="tpu_custom_call" | custom-call | tf_op jit(solution)/shard_map/final/pallas_call | solution.py:660
  (6 shorter events, 0.0 us)
Async XLA Ops:
  0.0 0.9 %copy-start = (f32[16,4096]{1,0:T(8,128)S(1)}, f32[16,4096]{1,0:T(8,128)}, u32[]{:S(2)}) copy-start(f32[16,4096]{1,0:T(8,128)} %refs_5_.1) | copy-start | bytes 786436
  1.0 1.0 %copy-start.2 = (f32[32,4096]{1,0:T(8,128)S(1)}, f32[32,4096]{1,0:T(8,128)}, u32[]{:S(2)}) copy-start(f32[32,4096]{1,0:T(8,128)} %refs_2_.4) | copy-start | bytes 1572868
  2.0 0.8 %copy-start.4 = (f32[3,4096]{1,0:T(4,128)S(1)}, f32[3,4096]{1,0:T(4,128)}, u32[]{:S(2)}) copy-start(f32[3,4096]{1,0:T(4,128)} %refs_6_.1) | copy-start | bytes 147460
  2.8 1.0 %copy-start.6 = (f32[32,32,84]{2,1,0:T(8,128)S(1)}, f32[32,32,84]{2,1,0:T(8,128)}, u32[]{:S(2)}) copy-start(f32[32,32,84]{2,1,0:T(8,128)} %param.11) | copy-start | bytes 1032196
  3.9 0.8 %copy-start.8 = (f32[3,32,85]{2,1,0:T(8,128)S(1)}, f32[3,32,85]{2,1,0:T(8,128)}, u32[]{:S(2)}) copy-start(f32[3,32,85]{2,1,0:T(8,128)} %param.12) | copy-start | bytes 97924
  4.7 21.2 %copy-start.5 = (f32[3,4096]{1,0:T(4,128)S(1)}, f32[3,4096]{1,0:T(4,128)}, u32[]{:S(2)}) copy-start(f32[3,4096]{1,0:T(4,128)} %refs_6_.1) | copy-start | bytes 147460
  4.7 21.2 %copy-start.9 = (s32[64,5]{0,1:T(8,128)S(1)}, s32[64,5]{0,1:T(8,128)}, u32[]{:S(2)}) copy-start(s32[64,5]{0,1:T(8,128)} %param.13) | copy-start | bytes 3844
  7.1 18.8 %copy-start.1 = (f32[16,4096]{1,0:T(8,128)S(1)}, f32[16,4096]{1,0:T(8,128)}, u32[]{:S(2)}) copy-start(f32[16,4096]{1,0:T(8,128)} %refs_5_.1) | copy-start | bytes 786436
  7.1 22.3 %copy-start.3 = (f32[32,4096]{1,0:T(8,128)S(1)}, f32[32,4096]{1,0:T(8,128)}, u32[]{:S(2)}) copy-start(f32[32,4096]{1,0:T(8,128)} %refs_2_.4) | copy-start | bytes 1572868
  7.1 1.7 %collective-permute-start = (f32[24,896]{1,0:T(8,128)S(1)}, f32[24,896]{1,0:T(8,128)S(1)}, u32[]{:S(2)}, u32[]{:S(2)}) collective-permute-start(f32[24,896]{1,0:T(8,128)S(1)} %get-tuple-element.21), channel_id=1, source_target_pairs={{0,1},{1,0},{2,3},{3,2},{4,5},{5,4},{6,7},{7,6},{8,9},{9,8},{10,11... | collective-permute-start | bytes 258056 | tf_op jit(solution)/shard_map/ppermute | solution.py:562
  8.8 2.5 %collective-permute-start.1 = (f32[2,8,128]{2,1,0:T(8,128)S(1)}, f32[2,8,128]{2,1,0:T(8,128)S(1)}, u32[]{:S(2)}, u32[]{:S(2)}) collective-permute-start(f32[2,8,128]{2,1,0:T(8,128)S(1)} %get-tuple-element.24.lower), channel_id=1, source_target_pairs={{0,2},{1,3},{2,0},{3,1},{4,6},{5,7},{6,4},{7,5},{8,10},{9,11},{10,... | collective-permute-start | bytes 24584 | tf_op jit(solution)/shard_map/ppermute | solution.py:562
  11.3 2.6 %collective-permute-start.2 = (f32[4,8,128]{2,1,0:T(8,128)S(1)}, f32[4,8,128]{2,1,0:T(8,128)S(1)}, u32[]{:S(2)}, u32[]{:S(2)}) collective-permute-start(f32[4,8,128]{2,1,0:T(8,128)S(1)} %join.4.lower), channel_id=1, source_target_pairs={{0,4},{1,5},{2,6},{3,7},{4,0},{5,1},{6,2},{7,3},{8,12},{9,13},{10,... | collective-permute-start | bytes 49160 | tf_op jit(solution)/shard_map/ppermute | solution.py:562
  13.9 7.3 %collective-permute-start.3 = (f32[8,8,128]{2,1,0:T(8,128)S(1)}, f32[8,8,128]{2,1,0:T(8,128)S(1)}, u32[]{:S(2)}, u32[]{:S(2)}) collective-permute-start(f32[8,8,128]{2,1,0:T(8,128)S(1)} %join.5.lower), channel_id=1, source_target_pairs={{0,8},{1,9},{2,10},{3,11},{4,12},{5,13},{6,14},{7,15},{8,0},{9,1},... | collective-permute-start | bytes 98312 | tf_op jit(solution)/shard_map/ppermute | solution.py:562
  15.2 8.1 %collective-permute-start.5 = (f32[24,896]{1,0:T(8,128)S(1)}, f32[24,896]{1,0:T(8,128)S(1)}, u32[]{:S(2)}, u32[]{:S(2)}) collective-permute-start(f32[24,896]{1,0:T(8,128)S(1)} %get-tuple-element.26), channel_id=1, source_target_pairs={{1,2},{3,4},{5,6},{7,8},{9,10},{11,12},{13,14},{15,16},{17,18},{19... | collective-permute-start | bytes 258056 | tf_op jit(solution)/shard_map/ppermute | solution.py:587
  21.2 11.7 %collective-permute-start.4 = (f32[16,8,128]{2,1,0:T(8,128)S(1)}, f32[16,8,128]{2,1,0:T(8,128)S(1)}, u32[]{:S(2)}, u32[]{:S(2)}) collective-permute-start(f32[16,8,128]{2,1,0:T(8,128)S(1)} %join.6.lower), channel_id=1, source_target_pairs={{0,16},{1,17},{2,18},{3,19},{4,20},{5,21},{6,22},{7,23},{8,24},{9,... | collective-permute-start | bytes 196616 | tf_op jit(solution)/shard_map/ppermute | solution.py:562
  23.4 9.6 %collective-permute-start.6 = (f32[24,128]{1,0:T(8,128)S(1)}, f32[24,128]{1,0:T(8,128)S(1)}, u32[]{:S(2)}, u32[]{:S(2)}) collective-permute-start(f32[24,128]{1,0:T(8,128)S(1)} %slice.4), channel_id=1, source_target_pairs={{0,1},{1,0},{2,3},{3,2},{4,5},{5,4},{6,7},{7,6},{8,9},{9,8},{10,11... | collective-permute-start | bytes 36872 | tf_op jit(solution)/shard_map/ppermute | solution.py:562
  25.9 3.5 %copy-start.7 = (s32[84,20]{0,1:T(8,128)S(1)}, s32[84,20]{0,1:T(8,128)}, u32[]{:S(2)}) copy-start(s32[84,20]{0,1:T(8,128)} %param.14) | copy-start | bytes 20164
  33.0 0.7 %copy-start.10 = (s32[1,32]{1,0:T(1,128)S(1)}, s32[1,32]{1,0:T(1,128)}, u32[]{:S(2)}) copy-start(s32[1,32]{1,0:T(1,128)} %refs_2_.5) | copy-start | bytes 388

commit v3 on v2

--- a/solution.py
+++ b/solution.py
@@ -6,6 +6,7 @@
 from jax.experimental import pallas as pl
 from jax.experimental.pallas import tpu as pltpu
 from jax.sharding import PartitionSpec as P
+
 
 LEVELS = 3
 REACH = 2
@@ -128,15 +129,30 @@
 
 
 def upward_kernel(
-    device, rhs, points, basis, transfer, prox,
+    device, rhs_hbm, points_hbm, basis_hbm, transfer_hbm, prox_hbm,
     c3, c2, c1, tile0, first, second, table_high, table_low,
-    padded, moved, *, leaf, rank, starts,
+    rhs, points, basis, transfer, prox, padded, moved, sems, *, leaf, rank, starts,
 ):
     vectors = rhs.shape[0]
     coords = points.shape[0]
     span = FAN * leaf
     group = FAN * rank
     outs = {1: c1, 2: c2, 3: c3}
+    copies = [
+        pltpu.make_async_copy(source, to, sems.at[i])
+        for i, (source, to) in enumerate(
+            (
+                (transfer_hbm, transfer),
+                (basis_hbm, basis),
+                (rhs_hbm, rhs),
+                (prox_hbm, prox),
+                (points_hbm, points),
+            )
+        )
+    ]
+    for copy in copies:
+        copy.start()
+    copies[0].wait()
 
     n_clusters = transfer.shape[1]
     padded[...] = jnp.zeros(padded.shape, F32)
@@ -162,6 +178,8 @@
             moved[t : t + FAN].reshape(group, LANES)
         )
 
+    for copy in copies[1:]:
+        copy.wait()
     for g in range(rhs.shape[1] // span):
         high, low = block_rows(basis, g * span, leaf)
         c3[:vectors, g * group : (g + 1) * group] = dot2(
@@ -256,33 +274,35 @@
     out[count:] = upper[...]
 
 
-def near_kernel(rhs, points, near, out, src, tgt, coef, mask, high, low, *, leaf, unroll):
-    n_points = rhs.shape[1]
+def near_kernel(rhs, points, near, out, src, tgt, coef, mask, high, low, *, leaf, begin, unroll):
     halo = REACH * leaf
-    count = n_points // halo
-    set_features(pad_rows(points[...]), src, tgt, 0)
-    coef[...] = stack2(rhs[...])
-    for at in range(0, n_points, 1024):
-        mask[:, at : at + 1024] = near_mask(near, at, 1024, leaf)
+    width = coef.shape[1]
+    count = width // halo - 2
+    lanes = slice(begin * halo, begin * halo + width)
+    set_features(pad_rows(points[:, lanes]), src, tgt, 0)
+    coef[...] = stack2(rhs[:, lanes])
+    for at in range(0, width, 512):
+        end = min(at + 512, width)
+        mask[:, at:end] = near_mask(near, begin * halo + at, end - at, leaf)
 
     def fill(g, carry):
-        begin = pl.multiple_of(g * halo, LANES)
+        row = pl.multiple_of(g * halo, LANES)
+        target = pl.multiple_of(row + halo, LANES)
         fill_block(
-            src, tgt, begin, pl.multiple_of(begin + halo, LANES), 3 * halo,
-            mask[:, pl.ds(pl.multiple_of(begin + halo, LANES), halo)], leaf,
+            src, tgt, row, target, 3 * halo, mask[:, pl.ds(target, halo)], leaf,
             high, low, pl.multiple_of(g * 3 * halo, LANES),
         )
         return carry
 
     def use(g, carry):
-        begin = pl.multiple_of(g * halo, LANES)
-        out[:, pl.ds(pl.multiple_of(begin + halo, LANES), halo)] = use_block(
-            coef, begin, 3 * halo, high, low, pl.multiple_of(g * 3 * halo, LANES)
+        row = pl.multiple_of(g * halo, LANES)
+        out[:, pl.ds(row, halo)] = use_block(
+            coef, row, 3 * halo, high, low, pl.multiple_of(g * 3 * halo, LANES)
         )
         return carry
 
-    lax.fori_loop(0, count - 2, fill, 0, unroll=unroll)
-    lax.fori_loop(0, count - 2, use, 0, unroll=unroll)
+    lax.fori_loop(0, count, fill, 0, unroll=unroll)
+    lax.fori_loop(0, count, use, 0, unroll=unroll)
 
 
 def near_mask(near, begin, width, leaf):
@@ -294,8 +314,8 @@
 
 
 def far_kernel(
-    c3, couple, basis, out, big_high, big_low, src, tgt, coef, mask, high, low,
-    *, leaf, rank, base, unroll,
+    device, c3, couple, basis, roots, out, big_high, big_low, usable,
+    src, tgt, coef, mask, high, low, *, leaf, rank, base, unroll, xor,
 ):
     group = FAN * rank
     vectors = out.shape[0]
@@ -329,11 +349,19 @@
     for g in range(basis.shape[1] // span):
         rows = slice(g * group, (g + 1) * group)
         big_high[rows, :], big_low[rows, :] = block_rows(basis, g * span, leaf)
+    n_roots = roots.shape[1]
+    listed = (jnp.broadcast_to(roots[...], (8, n_roots)) >= 0).astype(F32).astype(BF16)
+    for at in range(0, n_roots * rank, 512):
+        shape = (n_roots, 512)
+        source = at // rank + iota(shape, 1) // rank
+        if xor:
+            source = jnp.bitwise_xor(source, device[0])
+        usable[:, at : at + 512] = dot(listed, (iota(shape, 0) == source).astype(F32).astype(BF16))
 
 
 def edge_kernel(
-    device, first, second, c3, c2, rhs, points, near, couple,
-    near_edge, g3_edge, g2, ext, src, tgt, coef, high, low,
+    device, first, second, third, c3, c2, c1, rhs, points, near, couple,
+    near_edge, g3_edge, g2, g1, ext, src, tgt, coef, high, low,
     *, leaf, rank, starts,
 ):
     group = FAN * rank
@@ -348,8 +376,15 @@
     l2 = r3 + 3 * rim
     ln = l2 + n2 + 2 * rim
     rn = ln + 3 * halo
-
-    def rims(left, right):
+    one = rn + 3 * halo
+    here = 2 * rim + halo
+    own = first[:, here : here + group]
+    near_by = second[:, here : here + group]
+    beyond = second[:, here + group : here + 2 * group]
+
+    def rims(left, right, parts):
+        for i, part in enumerate(parts):
+            ext[:, one + i * group : one + (i + 1) * group] = part
         ext[:, l3 : l3 + rim] = left[:, :rim]
         ext[:, r3 + 2 * rim : r3 + 3 * rim] = right[:, :rim]
         ext[:, l2 : l2 + rim] = left[:, rim : 2 * rim]
@@ -359,11 +394,11 @@
 
     @pl.when(device[0] % 2 == 0)
     def _():
-        rims(second, first)
+        rims(second, first, (beyond, near_by, c1[...], own, third[...]))
 
     @pl.when(device[0] % 2 == 1)
     def _():
-        rims(first, second)
+        rims(first, second, (third[...], own, c1[...], near_by, beyond))
 
     ext[:, l3 + rim : l3 + 3 * rim] = c3[:, : 2 * rim]
     ext[:, r3 : r3 + 2 * rim] = c3[:, n3 - 2 * rim :]
@@ -382,6 +417,7 @@
             jobs.append((g3_edge, to * group, begin + i * group, 5 * group, rim, base3 + cluster))
     for q in range(n2 // group):
         jobs.append((g2, q * group, l2 + q * group, 5 * group, rim, base2 + q * FAN))
+    jobs.append((g1, 0, one, 5 * group, rim, starts[1] - 1))
     jobs.append((near_edge, 0, ln, 3 * halo, halo, 0))
     jobs.append((near_edge, halo, rn, 3 * halo, halo, n_leaves - 2))
     at = 0
@@ -399,18 +435,15 @@
 
 
 def final_kernel(
-    device, gathered, roots, tile0, c1, first, second, third, couple, near, near_edge,
-    g3, g3_edge, g2, table_high, table_low, big_high, big_low, out,
-    ext, src, tgt, coef, high, low, *, leaf, rank, starts, xor,
+    gathered, usable, tile0, near_low, near_high, near_edge, g3, g3_edge, g2, g1,
+    table_high, table_low, big_high, big_low, out,
+    ext, src, tgt, coef, high, low, *, leaf, rank, starts,
 ):
     group = FAN * rank
     vectors = out.shape[0]
-    me = device[0]
-    n_roots = roots.shape[1]
-    n_all = n_roots * rank
-    here = 2 * (2 * group) + REACH * leaf
+    n_all = usable.shape[1]
     block = iota((8, LANES), 1) // rank
-    for at in range(0, n_roots, FAN):
+    for at in range(0, n_all // rank, FAN):
         tiles = [jnp.zeros((8, LANES), F32)] * 3
         for j in range(FAN):
             value = gathered[at + j]
@@ -421,55 +454,23 @@
         lanes = slice(at * rank, at * rank + LANES)
         for i in range(3):
             ext[8 * i : 8 * i + 8, lanes] = tiles[i]
-    one = n_all
-
-    def order(parts):
-        for i, part in enumerate(parts):
-            ext[:, one + i * group : one + (i + 1) * group] = part
-
-    own = first[:, here : here + group]
-    near_by = second[:, here : here + group]
-    beyond = second[:, here + group : here + 2 * group]
-
-    @pl.when(me % 2 == 0)
-    def _():
-        order((beyond, near_by, c1[...], own, third[...]))
-
-    @pl.when(me % 2 == 1)
-    def _():
-        order((third[...], own, c1[...], near_by, beyond))
-
-    root = one + 5 * group
-    ext[vectors:, root : root + LANES] = pltpu.roll(tile0[...], rank, 1)
-    ext[:vectors, root : root + LANES] = jnp.zeros((vectors, LANES), F32)
-    set_features(ext[vectors:, :root], src, None, 0)
-    set_features(ext[vectors:, one + 2 * group : one + 3 * group], None, tgt, 0)
-    set_features(ext[vectors:, root : root + LANES], None, tgt, LANES)
-    listed = (jnp.broadcast_to(roots[...], (8, n_roots)) >= 0).astype(F32).astype(BF16)
+    set_features(ext[vectors:, :], src, None, 0)
+    set_features(pltpu.roll(tile0[...], rank, 1), None, tgt, 0)
     for at in range(0, n_all, 512):
-        shape = (n_roots, 512)
-        source = at // rank + iota(shape, 1) // rank
-        if xor:
-            source = jnp.bitwise_xor(source, me)
-        usable = dot(listed, (iota(shape, 0) == source).astype(F32).astype(BF16))
-        coef[:, at : at + 512] = stack2(ext[:vectors, at : at + 512] * usable[0:1])
-    coef[:, one:root] = stack2(ext[:vectors, one:root])
-    for at in range(0, n_all, 512):
-        fill_block(src, tgt, at, LANES, 512, None, rank, high, low, at)
-    fill_block(
-        src, tgt, one, 0, 5 * group, listed_mask(couple, 0, group, rank), rank, high, low, one
-    )
+        coef[:, at : at + 512] = stack2(
+            ext[:vectors, at : at + 512] * usable[0:1, at : at + 512]
+        )
+        fill_block(src, tgt, at, 0, 512, None, rank, high, low, at)
     f0 = jnp.zeros((vectors, LANES), F32)
     for at in range(0, n_all, 512):
         f0 = f0 + use_block(coef, at, 512, high, low, at)
-    g1 = use_block(coef, one, 5 * group, high, low, one)
 
     def down(above, level, q):
         begin = (starts[level] - 1) * rank + q * group
         rows = slice(begin, begin + group)
         return dot2(above, table_high[rows, :], table_low[rows, :], NT)
 
-    f1 = stack2(g1 + down(stack2(f0), 1, 0))
+    f1 = stack2(g1[...] + down(stack2(f0), 1, 0))
     f2 = []
     for q in range(FAN):
         f2.append(stack2(g2[:, q * group : (q + 1) * group] + down(f1, 2, q)))
@@ -487,15 +488,13 @@
         f3 = stack2(total + down(f2[q // FAN], 3, q))
         rows = slice(q * group, (q + 1) * group)
         value = dot2(f3, big_high[rows, :], big_low[rows, :])
-        if q == 0:
-            base = jnp.concatenate([near_edge[:, :halo], near[:, halo:span]], axis=1)
-        elif q == count - 1:
-            base = jnp.concatenate(
-                [near[:, q * span : (q + 1) * span - halo], near_edge[:, halo:]], axis=1
-            )
-        else:
-            base = near[:, q * span : (q + 1) * span]
-        out[:, q * span : (q + 1) * span] = base + value
+        out[:, q * span : (q + 1) * span] = value
+    n_low = near_low.shape[1]
+    n_high = near_high.shape[1]
+    out[:, :halo] += near_edge[:, :halo]
+    out[:, halo : halo + n_low] += near_low[...]
+    out[:, halo + n_low : halo + n_low + n_high] += near_high[...]
+    out[:, halo + n_low + n_high :] += near_edge[:, halo:]
 
 
 def largest_unroll(count, most):
@@ -527,15 +526,14 @@
     def shape(*dims, dtype=F32):
         return jax.ShapeDtypeStruct(dims, dtype)
 
-    def call(kernel, n_in, outs, scratch, name, mib, scalar=True):
+    def call(kernel, n_in, outs, scratch, mib, scalar=True, space=vmem):
         return pl.pallas_call(
             kernel,
             out_shape=outs,
-            in_specs=([smem] if scalar else []) + [vmem] * n_in,
+            in_specs=([smem] if scalar else []) + [space] * n_in,
             out_specs=jax.tree.map(lambda _: vmem, outs),
             scratch_shapes=scratch,
             compiler_params=pltpu.CompilerParams(vmem_limit_bytes=mib << 20),
-            name=name,
         )
 
     padded_clusters = -(-n_clusters // 8) * 8
@@ -553,76 +551,91 @@
             shape(n_clusters * rank, LANES, dtype=BF16),
             shape(n_clusters * rank, LANES, dtype=BF16),
         ),
-        [pltpu.VMEM((rank * rank, LANES), F32), pltpu.VMEM((padded_clusters, rank, LANES), F32)],
-        "upward",
+        [
+            *(
+                pltpu.VMEM(array.shape, F32)
+                for array in (rhs, points, leaf_basis, flat_transfer, flat_prox)
+            ),
+            pltpu.VMEM((rank * rank, LANES), F32),
+            pltpu.VMEM((padded_clusters, rank, LANES), F32),
+            pltpu.SemaphoreType.DMA((5,)),
+        ],
         16,
-    )(device, rhs, points, leaf_basis, flat_transfer, flat_prox)
+        space=pl.BlockSpec(memory_space=pltpu.HBM),
+    )(
+        device,
+        *(
+            pltpu.with_memory_space_constraint(array, pltpu.HBM)
+            for array in (rhs, points, leaf_basis, flat_transfer, flat_prox)
+        ),
+    )
 
     def swap(value, step):
         return lax.ppermute(value, "leaf", [(i, i ^ step) for i in range(count)])
 
     first = swap(to_first, 1)
     send, gathered = call(
-        middle_kernel,
-        3,
-        (shape(ROWS, width + group), shape(2, 8, LANES)),
-        [],
-        "middle",
-        2,
-        scalar=False,
+        middle_kernel, 3, (shape(ROWS, width + group), shape(2, 8, LANES)), [], 2, scalar=False
     )(first, to_second, tile0)
     xor = count & (count - 1) == 0
 
     def join(lower, upper):
         return call(
-            join_kernel, 2, shape(2 * lower.shape[0], 8, LANES), [], "join", 2, scalar=False
+            join_kernel, 2, shape(2 * lower.shape[0], 8, LANES), [], 2, scalar=False
         )(lower, upper)
 
+    pairs = [(i, i + 1) for i in range(1, count - 1, 2)]
+    second = lax.ppermute(send, "leaf", pairs + [(j, i) for i, j in pairs])
+    third = swap(second[:, width - group : width], 1)
     if xor:
         step = 2
         while step < count:
             other = swap(gathered, step)
-            if step == 2:
-                pairs = [(i, i + 1) for i in range(1, count - 1, 2)]
-                second = lax.ppermute(send, "leaf", pairs + [(j, i) for i, j in pairs])
-                third = swap(second[:, width - group : width], 1)
             gathered = join(gathered, other)
             step *= 2
     else:
         gathered = lax.all_gather(tile0, "leaf", axis=0)
-        pairs = [(i, i + 1) for i in range(1, count - 1, 2)]
-        second = lax.ppermute(send, "leaf", pairs + [(j, i) for i, j in pairs])
-        third = swap(second[:, width - group : width], 1)
-
-    n_near = n_points // halo - 2
-    near = call(
-        lambda *refs: near_kernel(*refs, leaf=leaf, unroll=largest_unroll(n_near, 16)),
-        3,
-        shape(vectors, n_points),
-        [
-            pltpu.VMEM((n_points, FEATS), BF16),
-            pltpu.VMEM((FEATS, n_points), BF16),
-            pltpu.VMEM((2 * vectors, n_points), BF16),
-            pltpu.VMEM((8, n_points), F32),
-            pltpu.VMEM((n_near * 3 * halo, LANES), BF16),
-            pltpu.VMEM((n_near * 3 * halo, LANES), BF16),
-        ],
-        "near",
-        16,
-        scalar=False,
-    )(rhs, points, near_t)
-
+
+    n_groups = n_points // halo
+
+    def near_part(begin, n_near):
+        lanes = (n_near + 2) * halo
+        return call(
+            lambda *refs: near_kernel(
+                *refs, leaf=leaf, begin=begin, unroll=largest_unroll(n_near, 16)
+            ),
+            3,
+            shape(vectors, n_near * halo),
+            [
+                pltpu.VMEM((lanes, FEATS), BF16),
+                pltpu.VMEM((FEATS, lanes), BF16),
+                pltpu.VMEM((2 * vectors, lanes), BF16),
+                pltpu.VMEM((8, lanes), F32),
+                pltpu.VMEM((n_near * 3 * halo, LANES), BF16),
+                pltpu.VMEM((n_near * 3 * halo, LANES), BF16),
+            ],
+            12,
+            scalar=False,
+        )(rhs, points, near_t)
+
+    half = (n_groups - 2) // 2
+    near_low = near_part(0, half)
+    near_high = near_part(half, n_groups - 2 - half)
+
+    n_all = count * rank
     n_far = FAN**2 - 4
     span = FAN * leaf
-    g3, big_high, big_low = call(
+    g3, big_high, big_low, usable = call(
         lambda *refs: far_kernel(
-            *refs, leaf=leaf, rank=rank, base=starts[3] - 1, unroll=largest_unroll(n_far, 12)
+            *refs, leaf=leaf, rank=rank, base=starts[3] - 1, unroll=largest_unroll(n_far, 12),
+            xor=xor,
         ),
-        3,
+        4,
         (
             shape(vectors, n3),
             shape(n_points // span * group, span, dtype=BF16),
             shape(n_points // span * group, span, dtype=BF16),
+            shape(8, n_all),
         ),
         [
             pltpu.VMEM((n3, FEATS), BF16),
@@ -632,17 +645,20 @@
             pltpu.VMEM((n_far * 5 * group, LANES), BF16),
             pltpu.VMEM((n_far * 5 * group, LANES), BF16),
         ],
-        "far",
-        16,
-        scalar=False,
-    )(c3, couple_t, leaf_basis)
-
-    n_ext = 6 * rim + n2 + 2 * rim + 6 * halo
-    n_rows = (4 + n2 // group) * 5 * group + 2 * 3 * halo
-    near_edge, g3_edge, g2 = call(
+        12,
+    )(device, c3, couple_t, leaf_basis, root_list)
+
+    n_ext = 6 * rim + n2 + 2 * rim + 6 * halo + 5 * group
+    n_rows = (5 + n2 // group) * 5 * group + 2 * 3 * halo
+    near_edge, g3_edge, g2, g1 = call(
         lambda *refs: edge_kernel(*refs, leaf=leaf, rank=rank, starts=starts),
-        8,
-        (shape(vectors, 2 * halo), shape(vectors, 2 * rim), shape(vectors, n2)),
+        10,
+        (
+            shape(vectors, 2 * halo),
+            shape(vectors, 2 * rim),
+            shape(vectors, n2),
+            shape(vectors, group),
+        ),
         [
             pltpu.VMEM((ROWS, n_ext), F32),
             pltpu.VMEM((n_ext, FEATS), BF16),
@@ -651,29 +667,28 @@
             pltpu.VMEM((n_rows, LANES), BF16),
             pltpu.VMEM((n_rows, LANES), BF16),
         ],
-        "edge",
-        16,
-    )(device, first, second, c3, c2, rhs, points, near_t, couple_t)
-
-    n_all = count * rank
-    n_top = n_all + 5 * group
+        12,
+    )(
+        device, first, second, third, c3, c2, c1, rhs, points, near_t, couple_t,
+    )
+
     return call(
-        lambda *refs: final_kernel(*refs, leaf=leaf, rank=rank, starts=starts, xor=xor),
-        17,
+        lambda *refs: final_kernel(*refs, leaf=leaf, rank=rank, starts=starts),
+        14,
         shape(vectors, n_points),
         [
-            pltpu.VMEM((ROWS, n_top + LANES), F32),
-            pltpu.VMEM((n_top, FEATS), BF16),
-            pltpu.VMEM((FEATS, 2 * LANES), BF16),
-            pltpu.VMEM((2 * vectors, n_top), BF16),
-            pltpu.VMEM((n_top, LANES), BF16),
-            pltpu.VMEM((n_top, LANES), BF16),
+            pltpu.VMEM((ROWS, n_all), F32),
+            pltpu.VMEM((n_all, FEATS), BF16),
+            pltpu.VMEM((FEATS, LANES), BF16),
+            pltpu.VMEM((2 * vectors, n_all), BF16),
+            pltpu.VMEM((n_all, LANES), BF16),
+            pltpu.VMEM((n_all, LANES), BF16),
         ],
-        "final",
-        16,
+        12,
+        scalar=False,
     )(
-        device, gathered, root_list, tile0, c1, first, second, third, couple_t, near, near_edge,
-        g3, g3_edge, g2, table_high, table_low, big_high, big_low,
+        gathered, usable, tile0, near_low, near_high, near_edge, g3, g3_edge, g2, g1,
+        table_high, table_low, big_high, big_low,
     )
 
 

time: 38.6 us -> 33.2 us (0.86)
  the two profiles are of different devices: /device:TPU:17 before, /device:TPU:0 now
where the time goes in v3:
time: 33.2 us; the launch traced here: 33 us
  Pallas kernels  15.2 us (46%)
  starting transfers between devices  10.9 us (33%)
  waiting for transfers between devices  6.08 us (18%)
  local copies, waits for them, and re-layouts  0.67 us (2%)
    ppermute x6, starting transfers between devices, swap(): return lax.ppermute(value, 'leaf', [(i, i ^ step) for i in range(count)])  10.2 us
    ppermute x6, waiting for transfers between devices, swap(): return lax.ppermute(value, 'leaf', [(i, i ^ step) for i in range(count)])  6.07 us
    pallas_call x1, Pallas kernels, body(): call(lambda *refs: final_kernel(*refs, leaf=leaf, rank=rank, starts=start...  4.53 us
    pallas_call x1, Pallas kernels, body(): call(lambda *refs: upward_kernel(*refs, leaf=leaf, rank=rank, starts=star...  4.01 us
    pallas_call x2, Pallas kernels, near_part(): call(lambda *refs: near_kernel(*refs, leaf=leaf, begin=begin, unroll=larg...  2.92 us
    pallas_call x1, Pallas kernels, body(): call(lambda *refs: far_kernel(*refs, leaf=leaf, rank=rank, base=starts[3]...  1.97 us
    pallas_call x1, Pallas kernels, body(): call(lambda *refs: edge_kernel(*refs, leaf=leaf, rank=rank, starts=starts...  1.8 us
    unnamed x12, local copies, waits for them, and re-layouts  0.67 us
  transfers between devices with their start and end apart: 7, of which 4 were waited for; matrix products, arithmetic and copies ran while one was open for 0% of the time, Pallas kernels for 20%

profile of v3, /device:TPU:0, one launch (start us, length us, event | category | flops | bytes accessed | tf_op | source)
XLA Modules:
  0.0 33.0 jit_solution(4656474187076932150)
XLA Ops:
  0.0 4.0 %shard_map.82 = (f32[24,2048]{1,0:T(8,128)S(1)}, f32[24,512]{1,0:T(8,128)S(1)}, f32[24,128]{1,0:T(8,128)S(1)}, f32[8,128]{1,0:T(8,128)S(1)}, f32[24,896]{1,0:T(8...) custom-call(s32[1]{0:T(128)} %bitcast.refs_0_, ...), custom_call_target="tpu_custom_call" | custom-call | tf_op jit(solution)/shard_map/pallas_call | solution.py:541
  4.0 0.0 copy-start
  4.0 0.6 %collective-permute-start = (f32[24,896]{1,0:T(8,128)S(1)}, f32[24,896]{1,0:T(8,128)S(1)}, u32[]{:S(2)}, u32[]{:S(2)}) collective-permute-start(f32[24,896]{1,0:T(8,128)S(1)} %get-tuple-element.23), channel_id=1, source_target_pairs={{0,1},{1,0},{2,3},{3,2},{4,5},{5,4},{6,7},{7,6},{8,9},{9,8},{10,11... | collective-permute-start | bytes 258056 | tf_op jit(solution)/shard_map/ppermute | solution.py:574
  4.6 0.9 %collective-permute-done.first.refs_1_ = f32[24,896]{1,0:T(8,128)S(1)} collective-permute-done((f32[24,896]{1,0:T(8,128)S(1)}, f32[24,896]{1,0:T(8,128)S(1)}, u32[]{:S(2)}, u32[]{:S(2)}) %collective-permute-start) | collective-permute-done | bytes 86048 | tf_op jit(solution)/shard_map/ppermute | solution.py:574
  5.5 2.9 %collective-permute-start.1 = (f32[2,8,128]{2,1,0:T(8,128)S(1)}, f32[2,8,128]{2,1,0:T(8,128)S(1)}, u32[]{:S(2)}, u32[]{:S(2)}) collective-permute-start(f32[2,8,128]{2,1,0:T(8,128)S(1)} %get-tuple-element.26.lower), channel_id=1, source_target_pairs={{0,2},{1,3},{2,0},{3,1},{4,6},{5,7},{6,4},{7,5},{8,10},{9,11},{10,... | collective-permute-start | bytes 24584 | tf_op jit(solution)/shard_map/ppermute | solution.py:574
  8.4 1.6 %collective-permute-done.1.upper = f32[2,8,128]{2,1,0:T(8,128)S(1)} collective-permute-done((f32[2,8,128]{2,1,0:T(8,128)S(1)}, f32[2,8,128]{2,1,0:T(8,128)S(1)}, u32[]{:S(2)}, u32[]{:S(2)}) %collective-permute-start.1) | collective-permute-done | bytes 8224 | tf_op jit(solution)/shard_map/ppermute | solution.py:574
  10.1 2.0 %collective-permute-start.2 = (f32[4,8,128]{2,1,0:T(8,128)S(1)}, f32[4,8,128]{2,1,0:T(8,128)S(1)}, u32[]{:S(2)}, u32[]{:S(2)}) collective-permute-start(f32[4,8,128]{2,1,0:T(8,128)S(1)} %shard_map.84.lower), channel_id=1, source_target_pairs={{0,4},{1,5},{2,6},{3,7},{4,0},{5,1},{6,2},{7,3},{8,12},{9,13},{10,... | collective-permute-start | bytes 49160 | tf_op jit(solution)/shard_map/ppermute | solution.py:574
  12.1 0.7 %collective-permute-start.5 = (f32[24,896]{1,0:T(8,128)S(1)}, f32[24,896]{1,0:T(8,128)S(1)}, u32[]{:S(2)}, u32[]{:S(2)}) collective-permute-start(f32[24,896]{1,0:T(8,128)S(1)} %get-tuple-element.29), channel_id=1, source_target_pairs={{1,2},{3,4},{5,6},{7,8},{9,10},{11,12},{13,14},{15,16},{17,18},{19... | collective-permute-start | bytes 258056 | tf_op jit(solution)/shard_map/ppermute | solution.py:588
  12.8 1.1 %collective-permute-done.2.upper = f32[4,8,128]{2,1,0:T(8,128)S(1)} collective-permute-done((f32[4,8,128]{2,1,0:T(8,128)S(1)}, f32[4,8,128]{2,1,0:T(8,128)S(1)}, u32[]{:S(2)}, u32[]{:S(2)}) %collective-permute-start.2) | collective-permute-done | bytes 16416 | tf_op jit(solution)/shard_map/ppermute | solution.py:574
  13.8 0.0 copy-start.2
  13.8 0.0 copy-start.4
  13.8 0.0 copy-start.1
  13.8 2.1 %collective-permute-start.3 = (f32[8,8,128]{2,1,0:T(8,128)S(1)}, f32[8,8,128]{2,1,0:T(8,128)S(1)}, u32[]{:S(2)}, u32[]{:S(2)}) collective-permute-start(f32[8,8,128]{2,1,0:T(8,128)S(1)} %shard_map.85.lower), channel_id=1, source_target_pairs={{0,8},{1,9},{2,10},{3,11},{4,12},{5,13},{6,14},{7,15},{8,0},{9,1},... | collective-permute-start | bytes 98312 | tf_op jit(solution)/shard_map/ppermute | solution.py:574
  16.0 2.5 %collective-permute-done.3.upper = f32[8,8,128]{2,1,0:T(8,128)S(1)} collective-permute-done((f32[8,8,128]{2,1,0:T(8,128)S(1)}, f32[8,8,128]{2,1,0:T(8,128)S(1)}, u32[]{:S(2)}, u32[]{:S(2)}) %collective-permute-start.3) | collective-permute-done | bytes 32800 | tf_op jit(solution)/shard_map/ppermute | solution.py:574
  18.4 2.6 %collective-permute-start.4 = (f32[16,8,128]{2,1,0:T(8,128)S(1)}, f32[16,8,128]{2,1,0:T(8,128)S(1)}, u32[]{:S(2)}, u32[]{:S(2)}) collective-permute-start(f32[16,8,128]{2,1,0:T(8,128)S(1)} %shard_map.86.lower), channel_id=1, source_target_pairs={{0,16},{1,17},{2,18},{3,19},{4,20},{5,21},{6,22},{7,23},{8,24},{9,... | collective-permute-start | bytes 196616 | tf_op jit(solution)/shard_map/ppermute | solution.py:574
  21.0 0.0 collective-permute-done.5.refs_2_
  21.0 0.0 collective-permute-start.6
  21.0 0.0 copy-done
  21.0 0.0 copy-done.2
  21.1 0.0 copy-done.4
  21.1 1.5 %shard_map.90.refs_4_ = f32[16,1920]{1,0:T(8,128)S(1)} custom-call(f32[16,4096]{1,0:T(8,128)S(1)} %copy-done, f32[3,4096]{1,0:T(4,128)S(1)} %copy-done.2, s32[5,64]{1,0:T(8,128)S(1)} %bitcast.7), custom_call_target="tpu_custom_call" | custom-call | tf_op jit(solution)/shard_map/pallas_call | solution.py:603
  22.5 0.0 copy-start.3
  22.5 1.5 %shard_map.89.refs_3_ = f32[16,1920]{1,0:T(8,128)S(1)} custom-call(f32[16,4096]{1,0:T(8,128)S(1)} %copy-done, f32[3,4096]{1,0:T(4,128)S(1)} %copy-done.2, s32[5,64]{1,0:T(8,128)S(1)} %bitcast.8), custom_call_target="tpu_custom_call" | custom-call | tf_op jit(solution)/shard_map/pallas_call | solution.py:603
  24.0 0.0 copy-start.5
  24.0 0.0 copy-done.1
  24.0 0.0 copy-done.3
  24.0 0.6 %copy-done.5 = s32[1,32]{1,0:T(1,128)S(1)} copy-done((s32[1,32]{1,0:T(1,128)S(1)}, s32[1,32]{1,0:T(1,128)}, u32[]{:S(2)}) %copy-start.5) | copy-done | bytes 152
  24.7 2.0 %shard_map.88 = (f32[16,2048]{1,0:T(8,128)S(1)}, bf16[2048,256]{1,0:T(8,128)(2,1)S(1)}, bf16[2048,256]{1,0:T(8,128)(2,1)S(1)}, f32[8,1024]{1,0:T(8,128)S(1)}) custom-call(s32[1]{0:T(128)} %bitcast.refs_0_, f32[24,2048]{1,0:T(8,128)S(1)} %get-tuple-element.27.refs_1_.refs_4_, s32[20,84]{1,0:T(8,128)S(1)} %bitcast.5, f32[32,4096]{1,0:T(8,128)S(1)} %copy-done.1, ...), custom_call_target="tpu_custom_call" | custom-call | tf_op jit(solution)/shard_map/pallas_call | solution.py:628
  26.6 0.0 collective-permute-done.6.refs_3_
  26.6 1.8 %shard_map.91 = (f32[16,256]{1,0:T(8,128)S(1)}, f32[16,512]{1,0:T(8,128)S(1)}, f32[16,512]{1,0:T(8,128)S(1)}, f32[16,128]{1,0:T(8,128)S(1)}) custom-call(s32[1]{0:T(128)} %bitcast.refs_0_, f32[24,896]{1,0:T(8,128)S(1)} %collective-permute-done.first.refs_1_, f32[24,896]{1,0:T(8,128)S(1)} %collective-permute-done.5.refs_2_, ...), custom_call_target="tpu_custom_call" | custom-call | tf_op jit(solution)/shard_map/pallas_call | solution.py:653
  28.4 0.0 collective-permute-done.4.upper
  28.5 4.5 %shard_map.92 = f32[16,4096]{1,0:T(8,128)} custom-call(f32[32,8,128]{2,1,0:T(8,128)S(1)} %shard_map.87.refs_0_, f32[8,1024]{1,0:T(8,128)S(1)} %get-tuple-element.28.refs_1_, f32[8,128]{1,0:T(8,128)S(1)} %get-tuple-element.25.tile0.refs_2_, f32[16,1920]{1,0:T(8,128)S(1)} %shard_map.89.refs_3_, f32[16,1920]{1,0:T(8,128)S(1)} %shard_map.90.refs_4_, ...), custom_call_target="tpu_custom_call" | custom-call | tf_op jit(solution)/shard_map/pallas_call | solution.py:675
  (6 shorter events, 0.0 us)
Async XLA Ops:
  4.0 17.0 %copy-start = (f32[16,4096]{1,0:T(8,128)S(1)}, f32[16,4096]{1,0:T(8,128)}, u32[]{:S(2)}) copy-start(f32[16,4096]{1,0:T(8,128)} %refs_7_.1) | copy-start | bytes 786436
  4.0 1.5 %collective-permute-start = (f32[24,896]{1,0:T(8,128)S(1)}, f32[24,896]{1,0:T(8,128)S(1)}, u32[]{:S(2)}, u32[]{:S(2)}) collective-permute-start(f32[24,896]{1,0:T(8,128)S(1)} %get-tuple-element.23), channel_id=1, source_target_pairs={{0,1},{1,0},{2,3},{3,2},{4,5},{5,4},{6,7},{7,6},{8,9},{9,8},{10,11... | collective-permute-start | bytes 258056 | tf_op jit(solution)/shard_map/ppermute | solution.py:574
  5.5 4.5 %collective-permute-start.1 = (f32[2,8,128]{2,1,0:T(8,128)S(1)}, f32[2,8,128]{2,1,0:T(8,128)S(1)}, u32[]{:S(2)}, u32[]{:S(2)}) collective-permute-start(f32[2,8,128]{2,1,0:T(8,128)S(1)} %get-tuple-element.26.lower), channel_id=1, source_target_pairs={{0,2},{1,3},{2,0},{3,1},{4,6},{5,7},{6,4},{7,5},{8,10},{9,11},{10,... | collective-permute-start | bytes 24584 | tf_op jit(solution)/shard_map/ppermute | solution.py:574
  10.1 3.8 %collective-permute-start.2 = (f32[4,8,128]{2,1,0:T(8,128)S(1)}, f32[4,8,128]{2,1,0:T(8,128)S(1)}, u32[]{:S(2)}, u32[]{:S(2)}) collective-permute-start(f32[4,8,128]{2,1,0:T(8,128)S(1)} %shard_map.84.lower), channel_id=1, source_target_pairs={{0,4},{1,5},{2,6},{3,7},{4,0},{5,1},{6,2},{7,3},{8,12},{9,13},{10,... | collective-permute-start | bytes 49160 | tf_op jit(solution)/shard_map/ppermute | solution.py:574
  12.1 8.9 %collective-permute-start.5 = (f32[24,896]{1,0:T(8,128)S(1)}, f32[24,896]{1,0:T(8,128)S(1)}, u32[]{:S(2)}, u32[]{:S(2)}) collective-permute-start(f32[24,896]{1,0:T(8,128)S(1)} %get-tuple-element.29), channel_id=1, source_target_pairs={{1,2},{3,4},{5,6},{7,8},{9,10},{11,12},{13,14},{15,16},{17,18},{19... | collective-permute-start | bytes 258056 | tf_op jit(solution)/shard_map/ppermute | solution.py:588
  13.8 7.2 %copy-start.2 = (f32[3,4096]{1,0:T(4,128)S(1)}, f32[3,4096]{1,0:T(4,128)}, u32[]{:S(2)}) copy-start(f32[3,4096]{1,0:T(4,128)} %refs_8_.1) | copy-start | bytes 147460
  13.8 7.2 %copy-start.4 = (s32[64,5]{0,1:T(8,128)S(1)}, s32[64,5]{0,1:T(8,128)}, u32[]{:S(2)}) copy-start(s32[64,5]{0,1:T(8,128)} %param.13) | copy-start | bytes 3844
  13.8 10.2 %copy-start.1 = (f32[32,4096]{1,0:T(8,128)S(1)}, f32[32,4096]{1,0:T(8,128)}, u32[]{:S(2)}) copy-start(f32[32,4096]{1,0:T(8,128)} %refs_3_.3) | copy-start | bytes 1572868
  13.8 4.6 %collective-permute-start.3 = (f32[8,8,128]{2,1,0:T(8,128)S(1)}, f32[8,8,128]{2,1,0:T(8,128)S(1)}, u32[]{:S(2)}, u32[]{:S(2)}) collective-permute-start(f32[8,8,128]{2,1,0:T(8,128)S(1)} %shard_map.85.lower), channel_id=1, source_target_pairs={{0,8},{1,9},{2,10},{3,11},{4,12},{5,13},{6,14},{7,15},{8,0},{9,1},... | collective-permute-start | bytes 98312 | tf_op jit(solution)/shard_map/ppermute | solution.py:574
  18.4 10.0 %collective-permute-start.4 = (f32[16,8,128]{2,1,0:T(8,128)S(1)}, f32[16,8,128]{2,1,0:T(8,128)S(1)}, u32[]{:S(2)}, u32[]{:S(2)}) collective-permute-start(f32[16,8,128]{2,1,0:T(8,128)S(1)} %shard_map.86.lower), channel_id=1, source_target_pairs={{0,16},{1,17},{2,18},{3,19},{4,20},{5,21},{6,22},{7,23},{8,24},{9,... | collective-permute-start | bytes 196616 | tf_op jit(solution)/shard_map/ppermute | solution.py:574
  21.0 5.6 %collective-permute-start.6 = (f32[24,128]{1,0:T(8,128)S(1)}, f32[24,128]{1,0:T(8,128)S(1)}, u32[]{:S(2)}, u32[]{:S(2)}) collective-permute-start(f32[24,128]{1,0:T(8,128)S(1)} %slice.4), channel_id=1, source_target_pairs={{0,1},{1,0},{2,3},{3,2},{4,5},{5,4},{6,7},{7,6},{8,9},{9,8},{10,11... | collective-permute-start | bytes 36872 | tf_op jit(solution)/shard_map/ppermute | solution.py:574
  22.5 1.5 %copy-start.3 = (s32[84,20]{0,1:T(8,128)S(1)}, s32[84,20]{0,1:T(8,128)}, u32[]{:S(2)}) copy-start(s32[84,20]{0,1:T(8,128)} %param.14) | copy-start | bytes 20164
  24.0 0.7 %copy-start.5 = (s32[1,32]{1,0:T(1,128)S(1)}, s32[1,32]{1,0:T(1,128)}, u32[]{:S(2)}) copy-start(s32[1,32]{1,0:T(1,128)} %refs_4_.1) | copy-start | bytes 388
